TPU v7x, 32 devices: a whole 2x2x4 slice. The times are simulated.
32 devices in a mesh: row: 8 (over y, x, core), rep: 4 (over z).
Axes of the slice: x: 2, y: 2, z: 4, core: 2. Of those that a mesh axis runs over, the one named last changes fastest.
Arguments:
- features: bfloat16 [8192, 512], P(('row', 'rep')), may hold values from -6 to 6
- tiles: bfloat16 [64, 8, 128, 128], P(('row', 'rep')), may hold values from -0.1875 to 0.1875
- columns: int32 [64, 8], P(('row', 'rep')), may hold values from 0 to 63, as said below
- w_aggregate: bfloat16 [512, 512], replicated, may hold values from -0.25 to 0.25
- w_self: bfloat16 [512, 512], replicated, may hold values from -0.25 to 0.25
- w_middle: bfloat16 [512, 512], replicated, may hold values from -0.25 to 0.25
- w_output: bfloat16 [512, 512], replicated, may hold values from -0.25 to 0.25
- cotangent: bfloat16 [8192, 512], P(('row', 'rep')), may hold values from -6 to 6
Outputs:
- updated: bfloat16 [8192, 512], P(('row', 'rep'))
- grad_features: bfloat16 [8192, 512], P(('row', 'rep'))
- grad_output: float32 [512, 512], P('rep')
- grad_middle: float32 [512, 512], P('rep')
- grad_aggregate: float32 [512, 512], P('rep')
- grad_self: float32 [512, 512], P('rep')
Inputs may be any that keep to these rules, and one draw needn't show every extreme that they name: `columns`: row group g holds row blocks g * 8 to (g + 1) * 8 - 1, for g < 8. Every column block named by a row block of group g lies in group g - 1, g or g + 1, taken modulo 8; every row block names each of these three groups at least once. Column blocks may repeat within a row block.
All inputs are finite; a program needn't handle non-finite values.
Results may differ from a plain program's by a relative error of at most 0.015.
Values may be sent and summed in bfloat16 or wider, within the bound.
No kernel may reach another device: no remote copies, remote signals or barrier semaphores. Data moves between devices by JAX's collectives and lax.ppermute only.
A program may use at most 192 MiB of HBM per device.

v0:
```python
import math

import jax
import jax.numpy as jnp
from jax import lax
from jax.experimental import pallas as pl
from jax.experimental.pallas import tpu as pltpu
from jax.sharding import PartitionSpec as P


BF = jnp.bfloat16
F32 = jnp.float32
VM = pl.BlockSpec(memory_space=pltpu.VMEM)
SM = pl.BlockSpec(memory_space=pltpu.SMEM)


def swap(value, axis, flip):
    count = lax.axis_size(axis)
    return lax.ppermute(value, axis, [(i, i ^ flip) for i in range(count)])


def swap_off(value):
    count = lax.axis_size("row")
    pairs = [(i, (i + 1) % count if i % 2 else (i - 1) % count) for i in range(count)]
    return lax.ppermute(value, "row", pairs)


def nbytes(shape, dtype):
    return math.prod(shape) * jnp.dtype(dtype).itemsize


def call(body, outs, ins, specs=None, flops=0):
    moved = sum(nbytes(o[0], o[1]) for o in outs) + sum(nbytes(i.shape, i.dtype) for i in ins)
    return pl.pallas_call(
        body,
        out_shape=[jax.ShapeDtypeStruct(shape, dtype) for shape, dtype in outs],
        in_specs=specs or [VM] * len(ins),
        out_specs=[VM] * len(outs),
        compiler_params=pltpu.CompilerParams(
            vmem_limit_bytes=min(moved + (8 << 20), 60 << 20)
        ),
        cost_estimate=pl.CostEstimate(flops=flops, bytes_accessed=moved, transcendentals=0),
    )(*ins)


def dot(left, right):
    return jnp.dot(left, right, preferred_element_type=F32)


def dot_nt(left, right):
    return lax.dot_general(left, right, (((1,), (1,)), ((), ())), preferred_element_type=F32)


def dot_tn(left, right):
    return lax.dot_general(left, right, (((0,), (0,)), ((), ())), preferred_element_type=F32)


def layer(features, tiles, columns, w_aggregate, w_self, w_middle, w_output, cotangent):
    blocks_dev, width_k, tile, _ = tiles.shape
    rows, width = features.shape
    half = width // 2
    groups = lax.axis_size("row")
    reps = lax.axis_size("rep")
    chips = groups // 2
    panel_blocks = reps * blocks_dev
    blocks = 3 * panel_blocks
    scale = 1.0 / math.sqrt(rows * groups * reps)
    level_rows = width // reps
    share_rows = 2 * level_rows // chips

    def half_of(offset):
        return pl.ds(pl.multiple_of(offset * half, half), half)

    def split_body(f_ref, mine_ref, other_ref):
        h = lax.axis_index("rep") & 1
        mine_ref[...] = f_ref[:, half_of(h)]
        other_ref[...] = f_ref[:, half_of(1 - h)]

    piece = ((rows, half), BF)
    own_mine, own_other = call(split_body, [piece, piece], [features])

    own = [own_mine] + [None] * (reps - 1)
    for d in range(reps - 1, 0, -1):
        own[d] = swap(own_other if d & 1 else own_mine, "rep", d)
    pair_columns = swap(columns, "rep", 1)
    pair_tiles = swap(tiles, "rep", 1)
    near = [swap(v, "row", 1) for v in own]
    far = [swap_off(v) for v in own]

    def build_body(t_ref, c_ref, a_ref, at_ref):
        g = lax.axis_index("row")
        r = lax.axis_index("rep")
        a_ref[...] = jnp.zeros_like(a_ref)
        at_ref[...] = jnp.zeros_like(at_ref)
        for b in range(blocks_dev):
            for k in range(width_k):
                c = c_ref[b, k]
                within = lax.rem(c, panel_blocks)
                group = lax.div(c, panel_blocks)
                slot = jnp.where(group == g, 0, jnp.where(group == (g ^ 1), 1, 2))
                level = lax.div(within, blocks_dev) ^ r
                index = (slot * reps + level) * blocks_dev + lax.rem(within, blocks_dev)
                t = t_ref[b, k]
                here = pl.ds(b * tile, tile)
                a_ref[index, here, :] += t
                at_ref[index, :, here] += t.T

    adj_shapes = [((blocks, rows, tile), BF), ((blocks, tile, rows), BF)]
    a_own, at_own = call(build_body, adj_shapes, [tiles, columns], [VM, SM])
    a_pair, at_pair = call(build_body, adj_shapes, [pair_tiles, pair_columns], [VM, SM])

    def early_body(f_ref, c_ref, ws_ref, wo_ref, self_ref, dso_ref):
        self_ref[...] = dot(f_ref[...], ws_ref[...])
        dso_ref[...] = dot_nt(c_ref[...], wo_ref[...])

    flops = 2 * rows * width * width
    wide = ((rows, width), F32)
    from_self, from_output = call(
        early_body, [wide, wide], [features, cotangent, w_self, w_output], flops=2 * flops
    )

    def add_pieces(a_ref, pieces, total):
        for slot, d, p_ref in pieces:
            first = (slot * reps + d) * blocks_dev
            lhs = jnp.concatenate([a_ref[first + u] for u in range(blocks_dev)], axis=1)
            total = total + dot(lhs, p_ref[...])
        return total

    late = [(2, d) for d in range(min(2, reps - 1), reps)]
    soon = [(s, d) for s in range(3) for d in range(reps) if (s, d) not in late]
    window = (own, near, far)

    def soon_body(ao_ref, ap_ref, *refs):
        pieces = [(s, d, ref) for (s, d), ref in zip(soon, refs)]
        zero = jnp.zeros((rows, half), F32)
        refs[-2][...] = add_pieces(ao_ref, pieces, zero)
        refs[-1][...] = add_pieces(ap_ref, pieces, zero)

    part = ((rows, half), F32)
    sum_own, sum_pair = call(
        soon_body, [part, part], [a_own, a_pair] + [window[s][d] for s, d in soon],
        flops=4 * len(soon) * rows * rows * half,
    )

    def late_body(ao_ref, ap_ref, so_ref, sp_ref, *refs):
        pieces = [(s, d, ref) for (s, d), ref in zip(late, refs)]
        refs[-2][...] = add_pieces(ao_ref, pieces, so_ref[...]).astype(BF)
        refs[-1][...] = add_pieces(ap_ref, pieces, sp_ref[...]).astype(BF)

    agg_mine, agg_send = call(
        late_body, [piece, piece],
        [a_own, a_pair, sum_own, sum_pair] + [window[s][d] for s, d in late],
        flops=4 * len(late) * rows * rows * half,
    )
    agg_other = swap(agg_send, "rep", 1)

    def chain_body(am_ref, ao_ref, self_ref, dso_ref, wa_ref, wm_ref,
                   dm_ref, do_ref, first_ref, second_ref, ds_ref, df_ref):
        h = lax.axis_index("rep") & 1
        wa_mine = wa_ref[half_of(h), :]
        wa_other = wa_ref[half_of(1 - h), :]
        pre_first = dot(am_ref[...], wa_mine) + dot(ao_ref[...], wa_other) + self_ref[...]
        sig = jax.nn.sigmoid(pre_first)
        slope_first = sig * (1.0 + pre_first * (1.0 - sig))
        first = (pre_first * sig).astype(BF)
        first_ref[...] = first
        pre_second = dot(first, wm_ref[...])
        sig = jax.nn.sigmoid(pre_second)
        second_ref[...] = (pre_second * sig).astype(BF)
        ds = (dso_ref[...] * (sig * (1.0 + pre_second * (1.0 - sig)))).astype(BF)
        ds_ref[...] = ds
        df = (dot_nt(ds, wm_ref[...]) * slope_first).astype(BF)
        df_ref[...] = df
        do_ref[...] = dot_nt(df, wa_other).astype(BF)
        dm_ref[...] = dot_nt(df, wa_mine).astype(BF)

    node = ((rows, width), BF)
    del_mine, del_send, first, second, delta_second, delta_first = call(
        chain_body, [piece, piece, node, node, node, node],
        [agg_mine, agg_other, from_self, from_output, w_aggregate, w_middle], flops=4 * flops,
    )
    del_pair = swap(del_send, "rep", 1)

    def grads_body(f_ref, c_ref, am_ref, ao_ref, first_ref, second_ref, ds_ref, df_ref, keep_ref, send_ref):
        core = lax.axis_index("row") & 1
        h = lax.axis_index("rep") & 1

        def put(number, where, value):
            value = value.astype(BF)

            @pl.when(core == number // 2)
            def _():
                keep_ref[number % 2, where, :] = value

            @pl.when(core != number // 2)
            def _():
                send_ref[number % 2, where, :] = value

        every = pl.ds(0, width)
        df = df_ref[...]
        put(0, every, dot_tn(second_ref[...], c_ref[...]))
        put(1, every, dot_tn(first_ref[...], ds_ref[...]))
        put(2, half_of(h), dot_tn(am_ref[...], df))
        put(2, half_of(1 - h), dot_tn(ao_ref[...], df))
        put(3, every, dot_tn(f_ref[...], df))

    pair_grads = ((2, width, width), BF)
    keep, send = call(
        grads_body, [pair_grads, pair_grads],
        [features, cotangent, agg_mine, agg_other, first, second, delta_second, delta_first],
        flops=4 * flops,
    )
    got = swap(send, "row", 1)

    def ends_body(f_ref, c_ref, second_ref, df_ref, wo_ref, ws_ref, up_ref, gs_ref):
        up_ref[...] = (f_ref[...].astype(F32) + dot(second_ref[...], wo_ref[...])).astype(BF)
        gs_ref[...] = c_ref[...].astype(F32) + dot_nt(df_ref[...], ws_ref[...])

    updated, grad_base = call(
        ends_body, [node, wide],
        [features, cotangent, second, delta_first, w_output, w_self], flops=2 * flops,
    )

    groups_of = (list(range(reps - 1, 1, -1)), [1, 0])
    order = groups_of[0] + groups_of[1]

    def messages(ao_ref, ap_ref, dm, dp, slot, d):
        here = pl.ds((slot * reps + d) * blocks_dev, blocks_dev)
        left = ao_ref[here].reshape(rows, rows)
        right = ap_ref[here].reshape(rows, rows)
        return (dot(left, dm) + dot(right, dp)).astype(BF)

    def spread(slot_lists):
        def body(ao_ref, ap_ref, dm_ref, dp_ref, *outs):
            dm = dm_ref[...]
            dp = dp_ref[...]
            for (slot, levels), out in zip(slot_lists, outs):
                for n, d in enumerate(levels):
                    out[n * rows : (n + 1) * rows] = messages(ao_ref, ap_ref, dm, dp, slot, d)

        return call(
            body, [((len(levels) * rows, half), BF) for _, levels in slot_lists],
            [at_own, at_pair, del_mine, del_pair],
            flops=4 * sum(len(v) for _, v in slot_lists) * rows * rows * half,
        )

    far_out = spread([(2, g) for g in groups_of])
    near_out, own_sum = spread([(1, order), (0, order)])
    far_in = [swap_off(v) for v in far_out]
    near_in = swap(near_out, "row", 1)

    home = [None] * reps
    for i, levels_here in enumerate(groups_of):
        base = len(groups_of[0]) if i else 0

        def add_body(own_ref, near_ref, far_ref, *outs, base=base):
            for n, out in enumerate(outs):
                there = pl.ds((base + n) * rows, rows)
                here = pl.ds(n * rows, rows)
                out[...] = (
                    own_ref[there].astype(F32)
                    + near_ref[there].astype(F32)
                    + far_ref[here].astype(F32)
                ).astype(out.dtype)

        sums = call(
            add_body, [part if d == 0 else piece for d in levels_here],
            [own_sum, near_in, far_in[i]],
        )
        for d, total in zip(levels_here, sums):
            home[d] = total if d == 0 else swap(total, "rep", d)

    def features_body(g_ref, *refs):
        h = lax.axis_index("rep") & 1
        out = refs[-1]
        for odd in range(2):
            total = g_ref[:, half_of(h ^ odd)]
            for d in range(odd, reps, 2):
                total = total + refs[d][...].astype(F32)
            out[:, half_of(h ^ odd)] = total.astype(BF)

    grad_features = call(features_body, [node], [grad_base] + home)[0]

    flips = [2 * d for d in range(chips)]
    cut = width // 2
    share = ((reps, share_rows, cut), BF)
    slab = ((2, level_rows, cut), BF)

    def share_at(number):
        start = lax.rem(number, chips // 2) * share_rows
        return number // (chips // 2), start

    def pack_body(k_ref, g_ref, *outs):
        r = lax.axis_index("rep")
        chip = lax.axis_index("row") // 2
        for e in range(reps):
            first = pl.multiple_of((r ^ e) * level_rows, level_rows)
            for n in range(chips):
                which, start = share_at(chip ^ n)
                here = pl.ds(pl.multiple_of(first + start, share_rows), share_rows)
                outs[n][e] = (
                    k_ref[which, here, :cut].astype(F32) + g_ref[which, here, :cut].astype(F32)
                ).astype(BF)
            here = pl.ds(first, level_rows)
            for i in range(2):
                outs[chips + e][i] = (
                    k_ref[i, here, cut:].astype(F32) + g_ref[i, here, cut:].astype(F32)
                ).astype(BF)

    packs = call(pack_body, [share] * chips + [slab] * reps, [keep, got])
    planes = [packs[0]] + [swap(packs[n], "row", flips[n]) for n in range(1, chips)]
    slabs = packs[chips:]
    slabs = [slabs[0]] + [swap(slabs[e], "rep", e) for e in range(1, reps)]

    def plane_body(*refs):
        ins, outs = refs[:chips], refs[chips:]
        for e in range(reps):
            total = ins[0][e].astype(F32)
            for n in range(1, chips):
                total = total + ins[n][e].astype(F32)
            outs[e][...] = total.astype(BF)

    small = ((share_rows, cut), BF)
    levels = call(plane_body, [small] * reps, planes)
    levels = [levels[0]] + [swap(levels[e], "rep", e) for e in range(1, reps)]

    def level_body(*refs):
        total = refs[0][...].astype(F32)
        for ref in refs[1:-1]:
            total = total + ref[...].astype(F32)
        refs[-1][...] = total.astype(BF)

    mine = call(level_body, [small], levels)[0]
    gathered = [mine] + [swap(mine, "row", flips[n]) for n in range(1, chips)]
    others = [swap(v, "row", 1) for v in gathered]

    slab_sum = call(level_body, [slab], slabs)[0]
    spans = [slab_sum] + [swap(slab_sum, "row", flips[n]) for n in range(1, chips)]

    def span_body(*refs):
        terms = [ref[...].astype(F32) for ref in refs[:-1]]
        while len(terms) > 1:
            terms = [a + b for a, b in zip(terms[::2], terms[1::2])]
        refs[-1][...] = terms[0].astype(BF)

    span = call(span_body, [slab], spans)[0]
    span_other = swap(span, "row", 1)

    def out_body(*refs):
        ours, theirs, outs = refs[:chips], refs[chips : 2 * chips], refs[2 * chips + 2 :]
        chip = lax.axis_index("row") // 2
        core = lax.axis_index("row") & 1

        def put(number, where, columns_here, value):
            for fixed in range(4):
                @pl.when(number == fixed)
                def _(fixed=fixed):
                    outs[fixed][where, columns_here] = value

        for side, source, slab_ref in (
            (core, ours, refs[2 * chips]), (1 - core, theirs, refs[2 * chips + 1])
        ):
            for n in range(chips):
                which, start = share_at(chip ^ n)
                here = pl.ds(pl.multiple_of(start, share_rows), share_rows)
                put(side * 2 + which, here, pl.ds(0, cut), source[n][...].astype(F32) * scale)
            for i in range(2):
                put(
                    side * 2 + i, pl.ds(0, level_rows), pl.ds(cut, width - cut),
                    slab_ref[i].astype(F32) * scale,
                )

    final = ((level_rows, width), F32)
    totals = call(out_body, [final] * 4, gathered + others + [span, span_other])
    return (updated, grad_features, *totals)


def solution(mesh):
    placed = (
        P(("row", "rep"), None),
        P(("row", "rep"), None, None, None),
        P(("row", "rep"), None),
        P(),
        P(),
        P(),
        P(),
        P(("row", "rep"), None),
    )
    return jax.shard_map(
        layer,
        mesh=mesh,
        in_specs=placed,
        out_specs=(
            P(("row", "rep"), None),
            P(("row", "rep"), None),
            P("rep", None),
            P("rep", None),
            P("rep", None),
            P("rep", None),
        ),
        check_vma=False,
    )
```

profile of v0, /device:TPU:0, one launch (start us, length us, event | category | flops | bytes accessed | tf_op | source)
XLA Modules:
  0.0 110.4 jit_solution(6770551118762179831)
XLA Ops:
  0.6 3.1 %collective-permute-start = (bf16[2,8,128,128]{3,2,1,0:T(8,128)(2,1)}, bf16[2,8,128,128]{3,2,1,0:T(8,128)(2,1)S(1)}, u32[]{:S(2)}, u32[]{:S(2)}) collective-permute-start(bf16[2,8,128,128]{3,2,1,0:T(8,128)(2,1)} %t_ref.1), channel_id=1, source_target_pairs={{0,1},{1,0},{2,3},{3,2},{4,5},{5,4},{6,7},{7,6},{8,9},{9,8},{10,11... | collective-permute-start | bytes 1572872 | tf_op jit(solution)/shard_map/ppermute | solution.py:19
  3.8 0.9 copy-done
  4.7 2.7 %collective-permute-start.3 = (bf16[256,256]{1,0:T(8,128)(2,1)S(1)}, bf16[256,256]{1,0:T(8,128)(2,1)S(1)}, u32[]{:S(2)}, u32[]{:S(2)}) collective-permute-start(bf16[256,256]{1,0:T(8,128)(2,1)S(1)} %get-tuple-element.54.refs_0_), channel_id=1, source_target_pairs={{0,2},{1,3},{2,0},{3,1},{4,6},{5,7},{6,4},{7,5},{8,10},{9,11},{10,... | collective-permute-start | bytes 393224 | tf_op jit(solution)/shard_map/ppermute | solution.py:19
  7.8 1.6 %collective-permute-start.1 = (s32[2,8]{1,0:T(2,128)}, s32[2,8]{1,0:T(2,128)S(1)}, u32[]{:S(2)}, u32[]{:S(2)}) collective-permute-start(s32[2,8]{1,0:T(2,128)} %c_ref.4), channel_id=1, source_target_pairs={{0,1},{1,0},{2,3},{3,2},{4,5},{5,4},{6,7},{7,6},{8,9},{9,8},{10,11... | collective-permute-start | bytes 200 | tf_op jit(solution)/shard_map/ppermute | solution.py:19
  9.4 12.5 %collective-permute-done.1.c_ref = s32[2,8]{1,0:T(2,128)S(1)} collective-permute-done((s32[2,8]{1,0:T(2,128)}, s32[2,8]{1,0:T(2,128)S(1)}, u32[]{:S(2)}, u32[]{:S(2)}) %collective-permute-start.1) | collective-permute-done | bytes 96 | tf_op jit(solution)/shard_map/ppermute | solution.py:19
  21.9 2.6 %collective-permute-start.9 = (bf16[256,256]{1,0:T(8,128)(2,1)S(1)}, bf16[256,256]{1,0:T(8,128)(2,1)S(1)}, u32[]{:S(2)}, u32[]{:S(2)}) collective-permute-start(bf16[256,256]{1,0:T(8,128)(2,1)S(1)} %get-tuple-element.54.refs_0_), channel_id=1, source_target_pairs={{0,28},{4,8},{8,4},{12,16},{16,12},{20,24},{24,20},{28,0},{1,29},{... | collective-permute-start | bytes 393224 | tf_op jit(solution)/shard_map/ppermute | solution.py:25
  24.5 2.0 %collective-permute-done.4.refs_3_ = bf16[256,256]{1,0:T(8,128)(2,1)S(1)} collective-permute-done((bf16[256,256]{1,0:T(8,128)(2,1)S(1)}, bf16[256,256]{1,0:T(8,128)(2,1)S(1)}, u32[]{:S(2)}, u32[]{:S(2)}) %collective-permute-start.4) | collective-permute-done | bytes 131104 | tf_op jit(solution)/shard_map/ppermute | solution.py:19
  26.5 1.0 collective-permute-start.10
  28.2 1.6 %collective-permute-start.11 = (bf16[256,256]{1,0:T(8,128)(2,1)S(1)}, bf16[256,256]{1,0:T(8,128)(2,1)S(1)}, u32[]{:S(2)}, u32[]{:S(2)}) collective-permute-start(bf16[256,256]{1,0:T(8,128)(2,1)S(1)} %collective-permute-done.3.refs_2_), channel_id=1, source_target_pairs={{0,28},{4,8},{8,4},{12,16},{16,12},{20,24},{24,20},{28,0},{1,29},{... | collective-permute-start | bytes 393224 | tf_op jit(solution)/shard_map/ppermute | solution.py:25
  29.8 1.1 collective-permute-start.12
  30.9 1.0 copy-done.5
  31.9 0.7 copy-done.8
  32.6 1.2 %shard_map.127 = (bf16[24,256,128]{2,1,0:T(8,128)(2,1)S(1)}, bf16[24,128,256]{2,1,0:T(8,128)(2,1)S(1)}) custom-call(bf16[2,8,128,128]{3,2,1,0:T(8,128)(2,1)S(1)} %copy-done.5, s32[2,8]{1,0:T(2,128)S(1)} %copy-done.8), custom_call_target="tpu_custom_call" | custom-call | bytes 3670080 | tf_op jit(solution)/shard_map/pallas_call | solution.py:34
  33.8 1.2 %shard_map.128 = (bf16[24,256,128]{2,1,0:T(8,128)(2,1)S(1)}, bf16[24,128,256]{2,1,0:T(8,128)(2,1)S(1)}) custom-call(bf16[2,8,128,128]{3,2,1,0:T(8,128)(2,1)S(1)} %collective-permute-done.t_ref, s32[2,8]{1,0:T(2,128)S(1)} %collective-permute-done.1.c_ref), custom_call_target="tpu_custom_call" | custom-call | bytes 3670080 | tf_op jit(solution)/shard_map/pallas_call | solution.py:34
  35.0 0.8 shard_map.130
  35.9 2.8 %collective-permute-done.12.refs_1_ = bf16[256,256]{1,0:T(8,128)(2,1)S(1)} collective-permute-done((bf16[256,256]{1,0:T(8,128)(2,1)S(1)}, bf16[256,256]{1,0:T(8,128)(2,1)S(1)}, u32[]{:S(2)}, u32[]{:S(2)}) %collective-permute-start.12) | collective-permute-done | bytes 131104 | tf_op jit(solution)/shard_map/ppermute | solution.py:25
  39.1 1.7 %collective-permute-start.13 = (bf16[256,256]{1,0:T(8,128)(2,1)S(1)}, bf16[256,256]{1,0:T(8,128)(2,1)S(1)}, u32[]{:S(2)}, u32[]{:S(2)}) collective-permute-start(bf16[256,256]{1,0:T(8,128)(2,1)S(1)} %get-tuple-element.59), channel_id=1, source_target_pairs={{0,1},{1,0},{2,3},{3,2},{4,5},{5,4},{6,7},{7,6},{8,9},{9,8},{10,11... | collective-permute-start | bytes 393224 | tf_op jit(solution)/shard_map/ppermute | solution.py:19
  41.2 2.9 %collective-permute-done.13.ao_ref = bf16[256,256]{1,0:T(8,128)(2,1)S(1)} collective-permute-done((bf16[256,256]{1,0:T(8,128)(2,1)S(1)}, bf16[256,256]{1,0:T(8,128)(2,1)S(1)}, u32[]{:S(2)}, u32[]{:S(2)}) %collective-permute-start.13) | collective-permute-done | bytes 131104 | tf_op jit(solution)/shard_map/ppermute | solution.py:19
  44.1 1.1 shard_map.133
  45.2 1.6 %shard_map.140 = (bf16[2,512,512]{2,1,0:T(8,128)(2,1)S(1)}, bf16[2,512,512]{2,1,0:T(8,128)(2,1)S(1)}) custom-call(bf16[256,512]{1,0:T(8,128)(2,1)S(1)} %copy-done.1, bf16[256,512]{1,0:T(8,128)(2,1)S(1)} %copy-done.4, bf16[256,256]{1,0:T(8,128)(2,1)S(1)} %get-tuple-element.58.am_ref, bf16[256,256]{1,0:T(8,128)(2,1)S(1)} %collective-permute-done.13.ao_ref, ...), custom_call_target="tpu_custom_call" | custom-call | flops 536870912 | bytes 3932160 | tf_op jit(solution)/shard_map/pallas_call | solution.py:34
  46.9 1.8 %collective-permute-start.14 = (bf16[256,256]{1,0:T(8,128)(2,1)S(1)}, bf16[256,256]{1,0:T(8,128)(2,1)S(1)}, u32[]{:S(2)}, u32[]{:S(2)}) collective-permute-start(bf16[256,256]{1,0:T(8,128)(2,1)S(1)} %get-tuple-element.69), channel_id=1, source_target_pairs={{0,1},{1,0},{2,3},{3,2},{4,5},{5,4},{6,7},{7,6},{8,9},{9,8},{10,11... | collective-permute-start | bytes 393224 | tf_op jit(solution)/shard_map/ppermute | solution.py:19
  48.7 4.1 %collective-permute-done.14.dp_ref = bf16[256,256]{1,0:T(8,128)(2,1)S(1)} collective-permute-done((bf16[256,256]{1,0:T(8,128)(2,1)S(1)}, bf16[256,256]{1,0:T(8,128)(2,1)S(1)}, u32[]{:S(2)}, u32[]{:S(2)}) %collective-permute-start.14) | collective-permute-done | bytes 131104 | tf_op jit(solution)/shard_map/ppermute | solution.py:19
  52.8 0.7 shard_map.135
  54.1 2.6 %collective-permute-start.18 = (bf16[512,256]{1,0:T(8,128)(2,1)S(1)}, bf16[512,256]{1,0:T(8,128)(2,1)S(1)}, u32[]{:S(2)}, u32[]{:S(2)}) collective-permute-start(bf16[512,256]{1,0:T(8,128)(2,1)S(1)} %get-tuple-element.75), channel_id=1, source_target_pairs={{0,28},{4,8},{8,4},{12,16},{16,12},{20,24},{24,20},{28,0},{1,29},{... | collective-permute-start | bytes 786440 | tf_op jit(solution)/shard_map/ppermute | solution.py:25
  57.0 1.8 %collective-permute-start.35 = (bf16[2,128,256]{2,1,0:T(8,128)(2,1)S(1)}, bf16[2,128,256]{2,1,0:T(8,128)(2,1)S(1)}, u32[]{:S(2)}, u32[]{:S(2)}) collective-permute-start(bf16[2,128,256]{2,1,0:T(8,128)(2,1)S(1)} %get-tuple-element.91), channel_id=1, source_target_pairs={{0,1},{1,0},{2,3},{3,2},{4,5},{5,4},{6,7},{7,6},{8,9},{9,8},{10,11... | collective-permute-start | bytes 393224 | tf_op jit(solution)/shard_map/ppermute | solution.py:19
  58.8 4.3 %collective-permute-start.36 = (bf16[2,128,256]{2,1,0:T(8,128)(2,1)S(1)}, bf16[2,128,256]{2,1,0:T(8,128)(2,1)S(1)}, u32[]{:S(2)}, u32[]{:S(2)}) collective-permute-start(bf16[2,128,256]{2,1,0:T(8,128)(2,1)S(1)} %get-tuple-element.92), channel_id=1, source_target_pairs={{0,2},{1,3},{2,0},{3,1},{4,6},{5,7},{6,4},{7,5},{8,10},{9,11},{10,... | collective-permute-start | bytes 393224 | tf_op jit(solution)/shard_map/ppermute | solution.py:19
  63.3 5.4 %collective-permute-start.37 = (bf16[2,128,256]{2,1,0:T(8,128)(2,1)S(1)}, bf16[2,128,256]{2,1,0:T(8,128)(2,1)S(1)}, u32[]{:S(2)}, u32[]{:S(2)}) collective-permute-start(bf16[2,128,256]{2,1,0:T(8,128)(2,1)S(1)} %get-tuple-element.93), channel_id=1, source_target_pairs={{0,3},{1,2},{2,1},{3,0},{4,7},{5,6},{6,5},{7,4},{8,11},{9,10},{10,... | collective-permute-start | bytes 393224 | tf_op jit(solution)/shard_map/ppermute | solution.py:19
  69.0 2.0 %collective-permute-start.23 = (bf16[4,64,256]{2,1,0:T(8,128)(2,1)S(1)}, bf16[4,64,256]{2,1,0:T(8,128)(2,1)S(1)}, u32[]{:S(2)}, u32[]{:S(2)}) collective-permute-start(bf16[4,64,256]{2,1,0:T(8,128)(2,1)S(1)} %get-tuple-element.84), channel_id=1, source_target_pairs={{0,16},{4,20},{8,24},{12,28},{16,0},{20,4},{24,8},{28,12},{1,17},{... | collective-permute-start | bytes 393224 | tf_op jit(solution)/shard_map/ppermute | solution.py:19
  71.1 1.6 %collective-permute-done.37.refs_3_ = bf16[2,128,256]{2,1,0:T(8,128)(2,1)S(1)} collective-permute-done((bf16[2,128,256]{2,1,0:T(8,128)(2,1)S(1)}, bf16[2,128,256]{2,1,0:T(8,128)(2,1)S(1)}, u32[]{:S(2)}, u32[]{:S(2)}) %collective-permute-start.37) | collective-permute-done | bytes 131104 | tf_op jit(solution)/shard_map/ppermute | solution.py:19
  72.6 1.3 %collective-permute-start.24 = (bf16[4,64,256]{2,1,0:T(8,128)(2,1)S(1)}, bf16[4,64,256]{2,1,0:T(8,128)(2,1)S(1)}, u32[]{:S(2)}, u32[]{:S(2)}) collective-permute-start(bf16[4,64,256]{2,1,0:T(8,128)(2,1)S(1)} %get-tuple-element.85), channel_id=1, source_target_pairs={{0,24},{4,28},{8,16},{12,20},{16,8},{20,12},{24,0},{28,4},{1,25},{... | collective-permute-start | bytes 393224 | tf_op jit(solution)/shard_map/ppermute | solution.py:19
  74.0 1.6 %collective-permute-start.38 = (bf16[2,128,256]{2,1,0:T(8,128)(2,1)S(1)}, bf16[2,128,256]{2,1,0:T(8,128)(2,1)S(1)}, u32[]{:S(2)}, u32[]{:S(2)}) collective-permute-start(bf16[2,128,256]{2,1,0:T(8,128)(2,1)S(1)} %shard_map.144.refs_0_), channel_id=1, source_target_pairs={{0,8},{4,12},{8,0},{12,4},{16,24},{20,28},{24,16},{28,20},{1,9},{5... | collective-permute-start | bytes 393224 | tf_op jit(solution)/shard_map/ppermute | solution.py:19
  76.3 1.3 %collective-permute-start.40 = (bf16[2,128,256]{2,1,0:T(8,128)(2,1)S(1)}, bf16[2,128,256]{2,1,0:T(8,128)(2,1)S(1)}, u32[]{:S(2)}, u32[]{:S(2)}) collective-permute-start(bf16[2,128,256]{2,1,0:T(8,128)(2,1)S(1)} %shard_map.144.refs_0_), channel_id=1, source_target_pairs={{0,24},{4,28},{8,16},{12,20},{16,8},{20,12},{24,0},{28,4},{1,25},{... | collective-permute-start | bytes 393224 | tf_op jit(solution)/shard_map/ppermute | solution.py:19
  77.6 5.1 %collective-permute-start.19 = (bf16[256,256]{1,0:T(8,128)(2,1)S(1)}, bf16[256,256]{1,0:T(8,128)(2,1)S(1)}, u32[]{:S(2)}, u32[]{:S(2)}) collective-permute-start(bf16[256,256]{1,0:T(8,128)(2,1)S(1)} %get-tuple-element.76), channel_id=1, source_target_pairs={{0,2},{1,3},{2,0},{3,1},{4,6},{5,7},{6,4},{7,5},{8,10},{9,11},{10,... | collective-permute-start | bytes 393224 | tf_op jit(solution)/shard_map/ppermute | solution.py:19
  82.8 1.2 %collective-permute-start.20 = (bf16[256,256]{1,0:T(8,128)(2,1)S(1)}, bf16[256,256]{1,0:T(8,128)(2,1)S(1)}, u32[]{:S(2)}, u32[]{:S(2)}) collective-permute-start(bf16[256,256]{1,0:T(8,128)(2,1)S(1)} %get-tuple-element.77), channel_id=1, source_target_pairs={{0,3},{1,2},{2,1},{3,0},{4,7},{5,6},{6,5},{7,4},{8,11},{9,10},{10,... | collective-permute-start | bytes 393224 | tf_op jit(solution)/shard_map/ppermute | solution.py:19
  84.5 1.7 %collective-permute-start.25 = (bf16[64,256]{1,0:T(8,128)(2,1)S(1)}, bf16[64,256]{1,0:T(8,128)(2,1)S(1)}, u32[]{:S(2)}, u32[]{:S(2)}) collective-permute-start(bf16[64,256]{1,0:T(8,128)(2,1)S(1)} %get-tuple-element.87), channel_id=1, source_target_pairs={{0,1},{1,0},{2,3},{3,2},{4,5},{5,4},{6,7},{7,6},{8,9},{9,8},{10,11... | collective-permute-start | bytes 98312 | tf_op jit(solution)/shard_map/ppermute | solution.py:19
  86.3 2.1 %collective-permute-start.26 = (bf16[64,256]{1,0:T(8,128)(2,1)S(1)}, bf16[64,256]{1,0:T(8,128)(2,1)S(1)}, u32[]{:S(2)}, u32[]{:S(2)}) collective-permute-start(bf16[64,256]{1,0:T(8,128)(2,1)S(1)} %get-tuple-element.88), channel_id=1, source_target_pairs={{0,2},{1,3},{2,0},{3,1},{4,6},{5,7},{6,4},{7,5},{8,10},{9,11},{10,... | collective-permute-start | bytes 98312 | tf_op jit(solution)/shard_map/ppermute | solution.py:19
  88.4 4.7 %collective-permute-done.25.refs_1_ = bf16[64,256]{1,0:T(8,128)(2,1)S(1)} collective-permute-done((bf16[64,256]{1,0:T(8,128)(2,1)S(1)}, bf16[64,256]{1,0:T(8,128)(2,1)S(1)}, u32[]{:S(2)}, u32[]{:S(2)}) %collective-permute-start.25) | collective-permute-done | bytes 32800 | tf_op jit(solution)/shard_map/ppermute | solution.py:19
  93.2 2.1 %collective-permute-done.26.refs_2_ = bf16[64,256]{1,0:T(8,128)(2,1)S(1)} collective-permute-done((bf16[64,256]{1,0:T(8,128)(2,1)S(1)}, bf16[64,256]{1,0:T(8,128)(2,1)S(1)}, u32[]{:S(2)}, u32[]{:S(2)}) %collective-permute-start.26) | collective-permute-done | bytes 32800 | tf_op jit(solution)/shard_map/ppermute | solution.py:19
  95.3 2.2 %collective-permute-start.27 = (bf16[64,256]{1,0:T(8,128)(2,1)S(1)}, bf16[64,256]{1,0:T(8,128)(2,1)S(1)}, u32[]{:S(2)}, u32[]{:S(2)}) collective-permute-start(bf16[64,256]{1,0:T(8,128)(2,1)S(1)} %get-tuple-element.89), channel_id=1, source_target_pairs={{0,3},{1,2},{2,1},{3,0},{4,7},{5,6},{6,5},{7,4},{8,11},{9,10},{10,... | collective-permute-start | bytes 98312 | tf_op jit(solution)/shard_map/ppermute | solution.py:19
  97.4 3.6 %collective-permute-done.27.refs_3_ = bf16[64,256]{1,0:T(8,128)(2,1)S(1)} collective-permute-done((bf16[64,256]{1,0:T(8,128)(2,1)S(1)}, bf16[64,256]{1,0:T(8,128)(2,1)S(1)}, u32[]{:S(2)}, u32[]{:S(2)}) %collective-permute-start.27) | collective-permute-done | bytes 32800 | tf_op jit(solution)/shard_map/ppermute | solution.py:19
  101.0 1.3 %collective-permute-start.28 = (bf16[64,256]{1,0:T(8,128)(2,1)S(1)}, bf16[64,256]{1,0:T(8,128)(2,1)S(1)}, u32[]{:S(2)}, u32[]{:S(2)}) collective-permute-start(bf16[64,256]{1,0:T(8,128)(2,1)S(1)} %shard_map.143.refs_0_), channel_id=1, source_target_pairs={{0,8},{4,12},{8,0},{12,4},{16,24},{20,28},{24,16},{28,20},{1,9},{5... | collective-permute-start | bytes 98312 | tf_op jit(solution)/shard_map/ppermute | solution.py:19
  102.3 2.2 %collective-permute-start.30 = (bf16[64,256]{1,0:T(8,128)(2,1)S(1)}, bf16[64,256]{1,0:T(8,128)(2,1)S(1)}, u32[]{:S(2)}, u32[]{:S(2)}) collective-permute-start(bf16[64,256]{1,0:T(8,128)(2,1)S(1)} %shard_map.143.refs_0_), channel_id=1, source_target_pairs={{0,24},{4,28},{8,16},{12,20},{16,8},{20,12},{24,0},{28,4},{1,25},{... | collective-permute-start | bytes 98312 | tf_op jit(solution)/shard_map/ppermute | solution.py:19
  104.6 0.8 collective-permute-done.28.refs_1_
  105.3 0.9 collective-permute-done.29.refs_2_
  106.2 1.0 collective-permute-done.30.refs_3_
  107.2 1.0 shard_map.134
  108.2 0.8 shard_map.139
  109.0 1.3 %shard_map.146 = (f32[128,512]{1,0:T(8,128)}, f32[128,512]{1,0:T(8,128)}, f32[128,512]{1,0:T(8,128)}, f32[128,512]{1,0:T(8,128)}) custom-call(bf16[64,256]{1,0:T(8,128)(2,1)S(1)} %shard_map.143.refs_0_, bf16[64,256]{1,0:T(8,128)(2,1)S(1)} %collective-permute-done.28.refs_1_, bf16[64,256]{1,0:T(8,128)(2,1)S(1)} %collective-permute-done.29.refs_2_, ...), custom_call_target="tpu_custom_call" | custom-call | bytes 1572864 | tf_op jit(solution)/shard_map/pallas_call | solution.py:34
  (74 shorter events, 5.0 us)
Async XLA Ops:
  0.6 29.1 %collective-permute-start = (bf16[2,8,128,128]{3,2,1,0:T(8,128)(2,1)}, bf16[2,8,128,128]{3,2,1,0:T(8,128)(2,1)S(1)}, u32[]{:S(2)}, u32[]{:S(2)}) collective-permute-start(bf16[2,8,128,128]{3,2,1,0:T(8,128)(2,1)} %t_ref.1), channel_id=1, source_target_pairs={{0,1},{1,0},{2,3},{3,2},{4,5},{5,4},{6,7},{7,6},{8,9},{9,8},{10,11... | collective-permute-start | bytes 1572872 | tf_op jit(solution)/shard_map/ppermute | solution.py:19
  4.7 17.2 %collective-permute-start.3 = (bf16[256,256]{1,0:T(8,128)(2,1)S(1)}, bf16[256,256]{1,0:T(8,128)(2,1)S(1)}, u32[]{:S(2)}, u32[]{:S(2)}) collective-permute-start(bf16[256,256]{1,0:T(8,128)(2,1)S(1)} %get-tuple-element.54.refs_0_), channel_id=1, source_target_pairs={{0,2},{1,3},{2,0},{3,1},{4,6},{5,7},{6,4},{7,5},{8,10},{9,11},{10,... | collective-permute-start | bytes 393224 | tf_op jit(solution)/shard_map/ppermute | solution.py:19
  7.4 17.1 %collective-permute-start.2 = (bf16[256,256]{1,0:T(8,128)(2,1)S(1)}, bf16[256,256]{1,0:T(8,128)(2,1)S(1)}, u32[]{:S(2)}, u32[]{:S(2)}) collective-permute-start(bf16[256,256]{1,0:T(8,128)(2,1)S(1)} %get-tuple-element.55), channel_id=1, source_target_pairs={{0,1},{1,0},{2,3},{3,2},{4,5},{5,4},{6,7},{7,6},{8,9},{9,8},{10,11... | collective-permute-start | bytes 393224 | tf_op jit(solution)/shard_map/ppermute | solution.py:19
  7.8 14.1 %collective-permute-start.1 = (s32[2,8]{1,0:T(2,128)}, s32[2,8]{1,0:T(2,128)S(1)}, u32[]{:S(2)}, u32[]{:S(2)}) collective-permute-start(s32[2,8]{1,0:T(2,128)} %c_ref.4), channel_id=1, source_target_pairs={{0,1},{1,0},{2,3},{3,2},{4,5},{5,4},{6,7},{7,6},{8,9},{9,8},{10,11... | collective-permute-start | bytes 200 | tf_op jit(solution)/shard_map/ppermute | solution.py:19
  9.4 17.1 %collective-permute-start.4 = (bf16[256,256]{1,0:T(8,128)(2,1)S(1)}, bf16[256,256]{1,0:T(8,128)(2,1)S(1)}, u32[]{:S(2)}, u32[]{:S(2)}) collective-permute-start(bf16[256,256]{1,0:T(8,128)(2,1)S(1)} %get-tuple-element.55), channel_id=1, source_target_pairs={{0,3},{1,2},{2,1},{3,0},{4,7},{5,6},{6,5},{7,4},{8,11},{9,10},{10,... | collective-permute-start | bytes 393224 | tf_op jit(solution)/shard_map/ppermute | solution.py:19
  21.9 5.6 %collective-permute-start.5 = (bf16[256,256]{1,0:T(8,128)(2,1)S(1)}, bf16[256,256]{1,0:T(8,128)(2,1)S(1)}, u32[]{:S(2)}, u32[]{:S(2)}) collective-permute-start(bf16[256,256]{1,0:T(8,128)(2,1)S(1)} %get-tuple-element.54.refs_0_), channel_id=1, source_target_pairs={{0,4},{4,0},{8,12},{12,8},{16,20},{20,16},{24,28},{28,24},{1,5},{5... | collective-permute-start | bytes 393224 | tf_op jit(solution)/shard_map/ppermute | solution.py:19
  21.9 6.2 %collective-permute-start.9 = (bf16[256,256]{1,0:T(8,128)(2,1)S(1)}, bf16[256,256]{1,0:T(8,128)(2,1)S(1)}, u32[]{:S(2)}, u32[]{:S(2)}) collective-permute-start(bf16[256,256]{1,0:T(8,128)(2,1)S(1)} %get-tuple-element.54.refs_0_), channel_id=1, source_target_pairs={{0,28},{4,8},{8,4},{12,16},{16,12},{20,24},{24,20},{28,0},{1,29},{... | collective-permute-start | bytes 393224 | tf_op jit(solution)/shard_map/ppermute | solution.py:25
  24.5 3.7 %collective-permute-start.7 = (bf16[256,256]{1,0:T(8,128)(2,1)S(1)}, bf16[256,256]{1,0:T(8,128)(2,1)S(1)}, u32[]{:S(2)}, u32[]{:S(2)}) collective-permute-start(bf16[256,256]{1,0:T(8,128)(2,1)S(1)} %collective-permute-done.3.refs_2_), channel_id=1, source_target_pairs={{0,4},{4,0},{8,12},{12,8},{16,20},{20,16},{24,28},{28,24},{1,5},{5... | collective-permute-start | bytes 393224 | tf_op jit(solution)/shard_map/ppermute | solution.py:19
  26.5 8.4 %collective-permute-start.10 = (bf16[256,256]{1,0:T(8,128)(2,1)S(1)}, bf16[256,256]{1,0:T(8,128)(2,1)S(1)}, u32[]{:S(2)}, u32[]{:S(2)}) collective-permute-start(bf16[256,256]{1,0:T(8,128)(2,1)S(1)} %collective-permute-done.2.refs_1_), channel_id=1, source_target_pairs={{0,28},{4,8},{8,4},{12,16},{16,12},{20,24},{24,20},{28,0},{1,29},{... | collective-permute-start | bytes 393224 | tf_op jit(solution)/shard_map/ppermute | solution.py:25
  27.6 7.4 %collective-permute-start.6 = (bf16[256,256]{1,0:T(8,128)(2,1)S(1)}, bf16[256,256]{1,0:T(8,128)(2,1)S(1)}, u32[]{:S(2)}, u32[]{:S(2)}) collective-permute-start(bf16[256,256]{1,0:T(8,128)(2,1)S(1)} %collective-permute-done.2.refs_1_), channel_id=1, source_target_pairs={{0,4},{4,0},{8,12},{12,8},{16,20},{20,16},{24,28},{28,24},{1,5},{5... | collective-permute-start | bytes 393224 | tf_op jit(solution)/shard_map/ppermute | solution.py:19
  28.1 6.8 %collective-permute-start.8 = (bf16[256,256]{1,0:T(8,128)(2,1)S(1)}, bf16[256,256]{1,0:T(8,128)(2,1)S(1)}, u32[]{:S(2)}, u32[]{:S(2)}) collective-permute-start(bf16[256,256]{1,0:T(8,128)(2,1)S(1)} %collective-permute-done.4.refs_3_), channel_id=1, source_target_pairs={{0,4},{4,0},{8,12},{12,8},{16,20},{20,16},{24,28},{28,24},{1,5},{5... | collective-permute-start | bytes 393224 | tf_op jit(solution)/shard_map/ppermute | solution.py:19
  28.2 7.7 %collective-permute-start.11 = (bf16[256,256]{1,0:T(8,128)(2,1)S(1)}, bf16[256,256]{1,0:T(8,128)(2,1)S(1)}, u32[]{:S(2)}, u32[]{:S(2)}) collective-permute-start(bf16[256,256]{1,0:T(8,128)(2,1)S(1)} %collective-permute-done.3.refs_2_), channel_id=1, source_target_pairs={{0,28},{4,8},{8,4},{12,16},{16,12},{20,24},{24,20},{28,0},{1,29},{... | collective-permute-start | bytes 393224 | tf_op jit(solution)/shard_map/ppermute | solution.py:25
  29.8 8.9 %collective-permute-start.12 = (bf16[256,256]{1,0:T(8,128)(2,1)S(1)}, bf16[256,256]{1,0:T(8,128)(2,1)S(1)}, u32[]{:S(2)}, u32[]{:S(2)}) collective-permute-start(bf16[256,256]{1,0:T(8,128)(2,1)S(1)} %collective-permute-done.4.refs_3_), channel_id=1, source_target_pairs={{0,28},{4,8},{8,4},{12,16},{16,12},{20,24},{24,20},{28,0},{1,29},{... | collective-permute-start | bytes 393224 | tf_op jit(solution)/shard_map/ppermute | solution.py:25
  38.7 2.1 %copy-start.1 = (bf16[256,512]{1,0:T(8,128)(2,1)S(1)}, bf16[256,512]{1,0:T(8,128)(2,1)}, u32[]{:S(2)}) copy-start(bf16[256,512]{1,0:T(8,128)(2,1)} %f_ref.7) | copy-start | bytes 786436
  38.7 2.1 %copy-start.2 = (bf16[512,512]{1,0:T(8,128)(2,1)S(1)}, bf16[512,512]{1,0:T(8,128)(2,1)}, u32[]{:S(2)}) copy-start(bf16[512,512]{1,0:T(8,128)(2,1)} %ws_ref.3) | copy-start | bytes 1572868
  38.7 2.1 %copy-start.3 = (bf16[512,512]{1,0:T(8,128)(2,1)S(1)}, bf16[512,512]{1,0:T(8,128)(2,1)}, u32[]{:S(2)}) copy-start(bf16[512,512]{1,0:T(8,128)(2,1)} %wo_ref.3) | copy-start | bytes 1572868
  38.7 2.1 %copy-start.4 = (bf16[256,512]{1,0:T(8,128)(2,1)S(1)}, bf16[256,512]{1,0:T(8,128)(2,1)}, u32[]{:S(2)}) copy-start(bf16[256,512]{1,0:T(8,128)(2,1)} %c_ref.7) | copy-start | bytes 786436
  39.0 5.1 %copy-start.6 = (bf16[512,512]{1,0:T(8,128)(2,1)S(1)}, bf16[512,512]{1,0:T(8,128)(2,1)}, u32[]{:S(2)}) copy-start(bf16[512,512]{1,0:T(8,128)(2,1)} %wa_ref.1) | copy-start | bytes 1572868
  39.1 5.1 %copy-start.7 = (bf16[512,512]{1,0:T(8,128)(2,1)S(1)}, bf16[512,512]{1,0:T(8,128)(2,1)}, u32[]{:S(2)}) copy-start(bf16[512,512]{1,0:T(8,128)(2,1)} %wm_ref.1) | copy-start | bytes 1572868
  39.1 5.0 %collective-permute-start.13 = (bf16[256,256]{1,0:T(8,128)(2,1)S(1)}, bf16[256,256]{1,0:T(8,128)(2,1)S(1)}, u32[]{:S(2)}, u32[]{:S(2)}) collective-permute-start(bf16[256,256]{1,0:T(8,128)(2,1)S(1)} %get-tuple-element.59), channel_id=1, source_target_pairs={{0,1},{1,0},{2,3},{3,2},{4,5},{5,4},{6,7},{7,6},{8,9},{9,8},{10,11... | collective-permute-start | bytes 393224 | tf_op jit(solution)/shard_map/ppermute | solution.py:19
  46.8 9.9 %collective-permute-start.21 = (bf16[2,512,512]{2,1,0:T(8,128)(2,1)S(1)}, bf16[2,512,512]{2,1,0:T(8,128)(2,1)S(1)}, u32[]{:S(2)}, u32[]{:S(2)}) collective-permute-start(bf16[2,512,512]{2,1,0:T(8,128)(2,1)S(1)} %get-tuple-element.81), channel_id=1, source_target_pairs={{0,4},{4,0},{8,12},{12,8},{16,20},{20,16},{24,28},{28,24},{1,5},{5... | collective-permute-start | bytes 3145736 | tf_op jit(solution)/shard_map/ppermute | solution.py:19
  46.9 5.9 %collective-permute-start.14 = (bf16[256,256]{1,0:T(8,128)(2,1)S(1)}, bf16[256,256]{1,0:T(8,128)(2,1)S(1)}, u32[]{:S(2)}, u32[]{:S(2)}) collective-permute-start(bf16[256,256]{1,0:T(8,128)(2,1)S(1)} %get-tuple-element.69), channel_id=1, source_target_pairs={{0,1},{1,0},{2,3},{3,2},{4,5},{5,4},{6,7},{7,6},{8,9},{9,8},{10,11... | collective-permute-start | bytes 393224 | tf_op jit(solution)/shard_map/ppermute | solution.py:19
  53.5 22.1 %collective-permute-start.15 = (bf16[1024,256]{1,0:T(8,128)(2,1)S(1)}, bf16[1024,256]{1,0:T(8,128)(2,1)S(1)}, u32[]{:S(2)}, u32[]{:S(2)}) collective-permute-start(bf16[1024,256]{1,0:T(8,128)(2,1)S(1)} %get-tuple-element.71), channel_id=1, source_target_pairs={{0,4},{4,0},{8,12},{12,8},{16,20},{20,16},{24,28},{28,24},{1,5},{5... | collective-permute-start | bytes 1572872 | tf_op jit(solution)/shard_map/ppermute | solution.py:19
  54.1 9.3 %collective-permute-start.18 = (bf16[512,256]{1,0:T(8,128)(2,1)S(1)}, bf16[512,256]{1,0:T(8,128)(2,1)S(1)}, u32[]{:S(2)}, u32[]{:S(2)}) collective-permute-start(bf16[512,256]{1,0:T(8,128)(2,1)S(1)} %get-tuple-element.75), channel_id=1, source_target_pairs={{0,28},{4,8},{8,4},{12,16},{16,12},{20,24},{24,20},{28,0},{1,29},{... | collective-permute-start | bytes 786440 | tf_op jit(solution)/shard_map/ppermute | solution.py:25
  56.6 17.3 %collective-permute-start.16 = (bf16[512,256]{1,0:T(8,128)(2,1)S(1)}, bf16[512,256]{1,0:T(8,128)(2,1)S(1)}, u32[]{:S(2)}, u32[]{:S(2)}) collective-permute-start(bf16[512,256]{1,0:T(8,128)(2,1)S(1)} %get-tuple-element.72), channel_id=1, source_target_pairs={{0,28},{4,8},{8,4},{12,16},{16,12},{20,24},{24,20},{28,0},{1,29},{... | collective-permute-start | bytes 786440 | tf_op jit(solution)/shard_map/ppermute | solution.py:25
  57.0 11.8 %collective-permute-start.35 = (bf16[2,128,256]{2,1,0:T(8,128)(2,1)S(1)}, bf16[2,128,256]{2,1,0:T(8,128)(2,1)S(1)}, u32[]{:S(2)}, u32[]{:S(2)}) collective-permute-start(bf16[2,128,256]{2,1,0:T(8,128)(2,1)S(1)} %get-tuple-element.91), channel_id=1, source_target_pairs={{0,1},{1,0},{2,3},{3,2},{4,5},{5,4},{6,7},{7,6},{8,9},{9,8},{10,11... | collective-permute-start | bytes 393224 | tf_op jit(solution)/shard_map/ppermute | solution.py:19
  58.8 10.2 %collective-permute-start.36 = (bf16[2,128,256]{2,1,0:T(8,128)(2,1)S(1)}, bf16[2,128,256]{2,1,0:T(8,128)(2,1)S(1)}, u32[]{:S(2)}, u32[]{:S(2)}) collective-permute-start(bf16[2,128,256]{2,1,0:T(8,128)(2,1)S(1)} %get-tuple-element.92), channel_id=1, source_target_pairs={{0,2},{1,3},{2,0},{3,1},{4,6},{5,7},{6,4},{7,5},{8,10},{9,11},{10,... | collective-permute-start | bytes 393224 | tf_op jit(solution)/shard_map/ppermute | solution.py:19
  63.3 9.3 %collective-permute-start.37 = (bf16[2,128,256]{2,1,0:T(8,128)(2,1)S(1)}, bf16[2,128,256]{2,1,0:T(8,128)(2,1)S(1)}, u32[]{:S(2)}, u32[]{:S(2)}) collective-permute-start(bf16[2,128,256]{2,1,0:T(8,128)(2,1)S(1)} %get-tuple-element.93), channel_id=1, source_target_pairs={{0,3},{1,2},{2,1},{3,0},{4,7},{5,6},{6,5},{7,4},{8,11},{9,10},{10,... | collective-permute-start | bytes 393224 | tf_op jit(solution)/shard_map/ppermute | solution.py:19
  68.8 7.5 %collective-permute-start.22 = (bf16[4,64,256]{2,1,0:T(8,128)(2,1)S(1)}, bf16[4,64,256]{2,1,0:T(8,128)(2,1)S(1)}, u32[]{:S(2)}, u32[]{:S(2)}) collective-permute-start(bf16[4,64,256]{2,1,0:T(8,128)(2,1)S(1)} %get-tuple-element.83), channel_id=1, source_target_pairs={{0,8},{4,12},{8,0},{12,4},{16,24},{20,28},{24,16},{28,20},{1,9},{5... | collective-permute-start | bytes 393224 | tf_op jit(solution)/shard_map/ppermute | solution.py:19
  69.0 8.6 %collective-permute-start.23 = (bf16[4,64,256]{2,1,0:T(8,128)(2,1)S(1)}, bf16[4,64,256]{2,1,0:T(8,128)(2,1)S(1)}, u32[]{:S(2)}, u32[]{:S(2)}) collective-permute-start(bf16[4,64,256]{2,1,0:T(8,128)(2,1)S(1)} %get-tuple-element.84), channel_id=1, source_target_pairs={{0,16},{4,20},{8,24},{12,28},{16,0},{20,4},{24,8},{28,12},{1,17},{... | collective-permute-start | bytes 393224 | tf_op jit(solution)/shard_map/ppermute | solution.py:19
  72.6 10.2 %collective-permute-start.24 = (bf16[4,64,256]{2,1,0:T(8,128)(2,1)S(1)}, bf16[4,64,256]{2,1,0:T(8,128)(2,1)S(1)}, u32[]{:S(2)}, u32[]{:S(2)}) collective-permute-start(bf16[4,64,256]{2,1,0:T(8,128)(2,1)S(1)} %get-tuple-element.85), channel_id=1, source_target_pairs={{0,24},{4,28},{8,16},{12,20},{16,8},{20,12},{24,0},{28,4},{1,25},{... | collective-permute-start | bytes 393224 | tf_op jit(solution)/shard_map/ppermute | solution.py:19
  74.0 10.1 %collective-permute-start.38 = (bf16[2,128,256]{2,1,0:T(8,128)(2,1)S(1)}, bf16[2,128,256]{2,1,0:T(8,128)(2,1)S(1)}, u32[]{:S(2)}, u32[]{:S(2)}) collective-permute-start(bf16[2,128,256]{2,1,0:T(8,128)(2,1)S(1)} %shard_map.144.refs_0_), channel_id=1, source_target_pairs={{0,8},{4,12},{8,0},{12,4},{16,24},{20,28},{24,16},{28,20},{1,9},{5... | collective-permute-start | bytes 393224 | tf_op jit(solution)/shard_map/ppermute | solution.py:19
  75.6 8.9 %collective-permute-start.39 = (bf16[2,128,256]{2,1,0:T(8,128)(2,1)S(1)}, bf16[2,128,256]{2,1,0:T(8,128)(2,1)S(1)}, u32[]{:S(2)}, u32[]{:S(2)}) collective-permute-start(bf16[2,128,256]{2,1,0:T(8,128)(2,1)S(1)} %shard_map.144.refs_0_), channel_id=1, source_target_pairs={{0,16},{4,20},{8,24},{12,28},{16,0},{20,4},{24,8},{28,12},{1,17},{... | collective-permute-start | bytes 393224 | tf_op jit(solution)/shard_map/ppermute | solution.py:19
  76.3 10.0 %collective-permute-start.40 = (bf16[2,128,256]{2,1,0:T(8,128)(2,1)S(1)}, bf16[2,128,256]{2,1,0:T(8,128)(2,1)S(1)}, u32[]{:S(2)}, u32[]{:S(2)}) collective-permute-start(bf16[2,128,256]{2,1,0:T(8,128)(2,1)S(1)} %shard_map.144.refs_0_), channel_id=1, source_target_pairs={{0,24},{4,28},{8,16},{12,20},{16,8},{20,12},{24,0},{28,4},{1,25},{... | collective-permute-start | bytes 393224 | tf_op jit(solution)/shard_map/ppermute | solution.py:19
  77.6 24.7 %collective-permute-start.19 = (bf16[256,256]{1,0:T(8,128)(2,1)S(1)}, bf16[256,256]{1,0:T(8,128)(2,1)S(1)}, u32[]{:S(2)}, u32[]{:S(2)}) collective-permute-start(bf16[256,256]{1,0:T(8,128)(2,1)S(1)} %get-tuple-element.76), channel_id=1, source_target_pairs={{0,2},{1,3},{2,0},{3,1},{4,6},{5,7},{6,4},{7,5},{8,10},{9,11},{10,... | collective-permute-start | bytes 393224 | tf_op jit(solution)/shard_map/ppermute | solution.py:19
  82.8 19.5 %collective-permute-start.20 = (bf16[256,256]{1,0:T(8,128)(2,1)S(1)}, bf16[256,256]{1,0:T(8,128)(2,1)S(1)}, u32[]{:S(2)}, u32[]{:S(2)}) collective-permute-start(bf16[256,256]{1,0:T(8,128)(2,1)S(1)} %get-tuple-element.77), channel_id=1, source_target_pairs={{0,3},{1,2},{2,1},{3,0},{4,7},{5,6},{6,5},{7,4},{8,11},{9,10},{10,... | collective-permute-start | bytes 393224 | tf_op jit(solution)/shard_map/ppermute | solution.py:19
  84.1 20.5 %collective-permute-start.17 = (bf16[256,256]{1,0:T(8,128)(2,1)S(1)}, bf16[256,256]{1,0:T(8,128)(2,1)S(1)}, u32[]{:S(2)}, u32[]{:S(2)}) collective-permute-start(bf16[256,256]{1,0:T(8,128)(2,1)S(1)} %get-tuple-element.74), channel_id=1, source_target_pairs={{0,1},{1,0},{2,3},{3,2},{4,5},{5,4},{6,7},{7,6},{8,9},{9,8},{10,11... | collective-permute-start | bytes 393224 | tf_op jit(solution)/shard_map/ppermute | solution.py:19
  84.5 8.6 %collective-permute-start.25 = (bf16[64,256]{1,0:T(8,128)(2,1)S(1)}, bf16[64,256]{1,0:T(8,128)(2,1)S(1)}, u32[]{:S(2)}, u32[]{:S(2)}) collective-permute-start(bf16[64,256]{1,0:T(8,128)(2,1)S(1)} %get-tuple-element.87), channel_id=1, source_target_pairs={{0,1},{1,0},{2,3},{3,2},{4,5},{5,4},{6,7},{7,6},{8,9},{9,8},{10,11... | collective-permute-start | bytes 98312 | tf_op jit(solution)/shard_map/ppermute | solution.py:19
  86.3 9.0 %collective-permute-start.26 = (bf16[64,256]{1,0:T(8,128)(2,1)S(1)}, bf16[64,256]{1,0:T(8,128)(2,1)S(1)}, u32[]{:S(2)}, u32[]{:S(2)}) collective-permute-start(bf16[64,256]{1,0:T(8,128)(2,1)S(1)} %get-tuple-element.88), channel_id=1, source_target_pairs={{0,2},{1,3},{2,0},{3,1},{4,6},{5,7},{6,4},{7,5},{8,10},{9,11},{10,... | collective-permute-start | bytes 98312 | tf_op jit(solution)/shard_map/ppermute | solution.py:19
  93.2 15.9 %collective-permute-start.41 = (bf16[2,128,256]{2,1,0:T(8,128)(2,1)S(1)}, bf16[2,128,256]{2,1,0:T(8,128)(2,1)S(1)}, u32[]{:S(2)}, u32[]{:S(2)}) collective-permute-start(bf16[2,128,256]{2,1,0:T(8,128)(2,1)S(1)} %shard_map.145.refs_8_), channel_id=1, source_target_pairs={{0,4},{4,0},{8,12},{12,8},{16,20},{20,16},{24,28},{28,24},{1,5},{5... | collective-permute-start | bytes 393224 | tf_op jit(solution)/shard_map/ppermute | solution.py:19
  95.3 5.7 %collective-permute-start.27 = (bf16[64,256]{1,0:T(8,128)(2,1)S(1)}, bf16[64,256]{1,0:T(8,128)(2,1)S(1)}, u32[]{:S(2)}, u32[]{:S(2)}) collective-permute-start(bf16[64,256]{1,0:T(8,128)(2,1)S(1)} %get-tuple-element.89), channel_id=1, source_target_pairs={{0,3},{1,2},{2,1},{3,0},{4,7},{5,6},{6,5},{7,4},{8,11},{9,10},{10,... | collective-permute-start | bytes 98312 | tf_op jit(solution)/shard_map/ppermute | solution.py:19
  101.0 4.3 %collective-permute-start.28 = (bf16[64,256]{1,0:T(8,128)(2,1)S(1)}, bf16[64,256]{1,0:T(8,128)(2,1)S(1)}, u32[]{:S(2)}, u32[]{:S(2)}) collective-permute-start(bf16[64,256]{1,0:T(8,128)(2,1)S(1)} %shard_map.143.refs_0_), channel_id=1, source_target_pairs={{0,8},{4,12},{8,0},{12,4},{16,24},{20,28},{24,16},{28,20},{1,9},{5... | collective-permute-start | bytes 98312 | tf_op jit(solution)/shard_map/ppermute | solution.py:19
  102.3 3.9 %collective-permute-start.29 = (bf16[64,256]{1,0:T(8,128)(2,1)S(1)}, bf16[64,256]{1,0:T(8,128)(2,1)S(1)}, u32[]{:S(2)}, u32[]{:S(2)}) collective-permute-start(bf16[64,256]{1,0:T(8,128)(2,1)S(1)} %shard_map.143.refs_0_), channel_id=1, source_target_pairs={{0,16},{4,20},{8,24},{12,28},{16,0},{20,4},{24,8},{28,12},{1,17},{... | collective-permute-start | bytes 98312 | tf_op jit(solution)/shard_map/ppermute | solution.py:19
  102.3 4.9 %collective-permute-start.30 = (bf16[64,256]{1,0:T(8,128)(2,1)S(1)}, bf16[64,256]{1,0:T(8,128)(2,1)S(1)}, u32[]{:S(2)}, u32[]{:S(2)}) collective-permute-start(bf16[64,256]{1,0:T(8,128)(2,1)S(1)} %shard_map.143.refs_0_), channel_id=1, source_target_pairs={{0,24},{4,28},{8,16},{12,20},{16,8},{20,12},{24,0},{28,4},{1,25},{... | collective-permute-start | bytes 98312 | tf_op jit(solution)/shard_map/ppermute | solution.py:19
  104.6 4.4 %collective-permute-start.31 = (bf16[64,256]{1,0:T(8,128)(2,1)S(1)}, bf16[64,256]{1,0:T(8,128)(2,1)S(1)}, u32[]{:S(2)}, u32[]{:S(2)}) collective-permute-start(bf16[64,256]{1,0:T(8,128)(2,1)S(1)} %shard_map.143.refs_0_), channel_id=1, source_target_pairs={{0,4},{4,0},{8,12},{12,8},{16,20},{20,16},{24,28},{28,24},{1,5},{5... | collective-permute-start | bytes 98312 | tf_op jit(solution)/shard_map/ppermute | solution.py:19
  105.3 3.7 %collective-permute-start.32 = (bf16[64,256]{1,0:T(8,128)(2,1)S(1)}, bf16[64,256]{1,0:T(8,128)(2,1)S(1)}, u32[]{:S(2)}, u32[]{:S(2)}) collective-permute-start(bf16[64,256]{1,0:T(8,128)(2,1)S(1)} %collective-permute-done.28.refs_1_), channel_id=1, source_target_pairs={{0,4},{4,0},{8,12},{12,8},{16,20},{20,16},{24,28},{28,24},{1,5},{5... | collective-permute-start | bytes 98312 | tf_op jit(solution)/shard_map/ppermute | solution.py:19
  106.2 2.8 %collective-permute-start.33 = (bf16[64,256]{1,0:T(8,128)(2,1)S(1)}, bf16[64,256]{1,0:T(8,128)(2,1)S(1)}, u32[]{:S(2)}, u32[]{:S(2)}) collective-permute-start(bf16[64,256]{1,0:T(8,128)(2,1)S(1)} %collective-permute-done.29.refs_2_), channel_id=1, source_target_pairs={{0,4},{4,0},{8,12},{12,8},{16,20},{20,16},{24,28},{28,24},{1,5},{5... | collective-permute-start | bytes 98312 | tf_op jit(solution)/shard_map/ppermute | solution.py:19
  107.2 1.8 %collective-permute-start.34 = (bf16[64,256]{1,0:T(8,128)(2,1)S(1)}, bf16[64,256]{1,0:T(8,128)(2,1)S(1)}, u32[]{:S(2)}, u32[]{:S(2)}) collective-permute-start(bf16[64,256]{1,0:T(8,128)(2,1)S(1)} %collective-permute-done.30.refs_3_), channel_id=1, source_target_pairs={{0,4},{4,0},{8,12},{12,8},{16,20},{20,16},{24,28},{28,24},{1,5},{5... | collective-permute-start | bytes 98312 | tf_op jit(solution)/shard_map/ppermute | solution.py:19
  (3 other events, 2.7 us)
where the time goes:
time: 111 us; the launch traced here: 110 us
  starting transfers between devices  55.6 us (50%)
  waiting for transfers between devices  39.6 us (36%)
  Pallas kernels  11.5 us (10%)
  local copies, waits for them, and re-layouts  2.7 us (2%)
    ppermute x36, starting transfers between devices, swap(): return lax.ppermute(value, axis, [(i, i ^ flip) for i in range(count)])  46.7 us
    ppermute x36, waiting for transfers between devices, swap(): return lax.ppermute(value, axis, [(i, i ^ flip) for i in range(count)])  36.4 us
    pallas_call x20, Pallas kernels, call(): pl.pallas_call(body, out_shape=[jax.ShapeDtypeStruct(shape, dtype) for sh...  11.5 us
    ppermute x6, starting transfers between devices, swap_off(): return lax.ppermute(value, 'row', pairs)  8.95 us
    ppermute x6, waiting for transfers between devices, swap_off(): return lax.ppermute(value, 'row', pairs)  3.21 us
    unnamed x18, local copies, waits for them, and re-layouts  2.7 us
  transfers between devices with their start and end apart: 42, of which 15 were waited for; matrix products, arithmetic and copies ran while one was open for 0% of the time, Pallas kernels for 7%

commit v1 on v0

--- a/solution.py
+++ b/solution.py
@@ -23,6 +23,10 @@
     count = lax.axis_size("row")
     pairs = [(i, (i + 1) % count if i % 2 else (i - 1) % count) for i in range(count)]
     return lax.ppermute(value, "row", pairs)
+
+
+def span_flips(chips):
+    return [2 << t for t in range(chips.bit_length() - 1)]
 
 
 def nbytes(shape, dtype):
@@ -87,27 +91,36 @@
     near = [swap(v, "row", 1) for v in own]
     far = [swap_off(v) for v in own]
 
-    def build_body(t_ref, c_ref, a_ref, at_ref):
-        g = lax.axis_index("row")
-        r = lax.axis_index("rep")
-        a_ref[...] = jnp.zeros_like(a_ref)
-        at_ref[...] = jnp.zeros_like(at_ref)
-        for b in range(blocks_dev):
-            for k in range(width_k):
-                c = c_ref[b, k]
-                within = lax.rem(c, panel_blocks)
-                group = lax.div(c, panel_blocks)
-                slot = jnp.where(group == g, 0, jnp.where(group == (g ^ 1), 1, 2))
-                level = lax.div(within, blocks_dev) ^ r
-                index = (slot * reps + level) * blocks_dev + lax.rem(within, blocks_dev)
-                t = t_ref[b, k]
-                here = pl.ds(b * tile, tile)
-                a_ref[index, here, :] += t
-                at_ref[index, :, here] += t.T
-
-    adj_shapes = [((blocks, rows, tile), BF), ((blocks, tile, rows), BF)]
-    a_own, at_own = call(build_body, adj_shapes, [tiles, columns], [VM, SM])
-    a_pair, at_pair = call(build_body, adj_shapes, [pair_tiles, pair_columns], [VM, SM])
+    def build_body(turned):
+        def body(t_ref, c_ref, *outs):
+            g = lax.axis_index("row")
+            r = lax.axis_index("rep")
+            for out in outs:
+                out[...] = jnp.zeros_like(out)
+            for b in range(blocks_dev):
+                for k in range(width_k):
+                    c = c_ref[b, k]
+                    within = lax.rem(c, panel_blocks)
+                    group = lax.div(c, panel_blocks)
+                    slot = jnp.where(group == g, 0, jnp.where(group == (g ^ 1), 1, 2))
+                    level = lax.div(within, blocks_dev) ^ r
+                    index = (slot * reps + level) * blocks_dev + lax.rem(within, blocks_dev)
+                    t = t_ref[b, k]
+                    here = pl.ds(b * tile, tile)
+                    for out, turn in zip(outs, turned):
+                        if turn:
+                            out[index, :, here] += t.T
+                        else:
+                            out[index, here, :] += t
+
+        return body
+
+    plain = ((blocks, rows, tile), BF)
+    turned = ((blocks, tile, rows), BF)
+    a_own, at_own = call(build_body((False, True)), [plain, turned], [tiles, columns], [VM, SM])
+    pair = [pair_tiles, pair_columns]
+    a_pair = call(build_body((False,)), [plain], pair, [VM, SM])[0]
+    at_pair = call(build_body((True,)), [turned], pair, [VM, SM])[0]
 
     def early_body(f_ref, c_ref, ws_ref, wo_ref, self_ref, dso_ref):
         self_ref[...] = dot(f_ref[...], ws_ref[...])
@@ -119,39 +132,19 @@
         early_body, [wide, wide], [features, cotangent, w_self, w_output], flops=2 * flops
     )
 
-    def add_pieces(a_ref, pieces, total):
-        for slot, d, p_ref in pieces:
-            first = (slot * reps + d) * blocks_dev
-            lhs = jnp.concatenate([a_ref[first + u] for u in range(blocks_dev)], axis=1)
+    window = own + near + far
+
+    def sum_body(a_ref, *refs):
+        total = jnp.zeros((rows, half), F32)
+        for n, p_ref in enumerate(refs[:-1]):
+            lhs = jnp.concatenate([a_ref[n * blocks_dev + u] for u in range(blocks_dev)], axis=1)
             total = total + dot(lhs, p_ref[...])
-        return total
-
-    late = [(2, d) for d in range(min(2, reps - 1), reps)]
-    soon = [(s, d) for s in range(3) for d in range(reps) if (s, d) not in late]
-    window = (own, near, far)
-
-    def soon_body(ao_ref, ap_ref, *refs):
-        pieces = [(s, d, ref) for (s, d), ref in zip(soon, refs)]
-        zero = jnp.zeros((rows, half), F32)
-        refs[-2][...] = add_pieces(ao_ref, pieces, zero)
-        refs[-1][...] = add_pieces(ap_ref, pieces, zero)
+        refs[-1][...] = total.astype(BF)
 
     part = ((rows, half), F32)
-    sum_own, sum_pair = call(
-        soon_body, [part, part], [a_own, a_pair] + [window[s][d] for s, d in soon],
-        flops=4 * len(soon) * rows * rows * half,
-    )
-
-    def late_body(ao_ref, ap_ref, so_ref, sp_ref, *refs):
-        pieces = [(s, d, ref) for (s, d), ref in zip(late, refs)]
-        refs[-2][...] = add_pieces(ao_ref, pieces, so_ref[...]).astype(BF)
-        refs[-1][...] = add_pieces(ap_ref, pieces, sp_ref[...]).astype(BF)
-
-    agg_mine, agg_send = call(
-        late_body, [piece, piece],
-        [a_own, a_pair, sum_own, sum_pair] + [window[s][d] for s, d in late],
-        flops=4 * len(late) * rows * rows * half,
-    )
+    work = 2 * len(window) * rows * rows * half
+    agg_send = call(sum_body, [piece], [a_pair] + window, flops=work)[0]
+    agg_mine = call(sum_body, [piece], [a_own] + window, flops=work)[0]
     agg_other = swap(agg_send, "rep", 1)
 
     def chain_body(am_ref, ao_ref, self_ref, dso_ref, wa_ref, wm_ref,
@@ -181,36 +174,30 @@
     )
     del_pair = swap(del_send, "rep", 1)
 
-    def grads_body(f_ref, c_ref, am_ref, ao_ref, first_ref, second_ref, ds_ref, df_ref, keep_ref, send_ref):
-        core = lax.axis_index("row") & 1
-        h = lax.axis_index("rep") & 1
-
-        def put(number, where, value):
-            value = value.astype(BF)
-
-            @pl.when(core == number // 2)
+    def grads_body(sent):
+        def body(f_ref, c_ref, am_ref, ao_ref, first_ref, second_ref, ds_ref, df_ref, out_ref):
+            core = lax.axis_index("row") & 1
+            h = lax.axis_index("rep") & 1
+
+            @pl.when(core == (1 if sent else 0))
             def _():
-                keep_ref[number % 2, where, :] = value
-
-            @pl.when(core != number // 2)
+                out_ref[0] = dot_tn(second_ref[...], c_ref[...]).astype(BF)
+                out_ref[1] = dot_tn(first_ref[...], ds_ref[...]).astype(BF)
+
+            @pl.when(core == (0 if sent else 1))
             def _():
-                send_ref[number % 2, where, :] = value
-
-        every = pl.ds(0, width)
-        df = df_ref[...]
-        put(0, every, dot_tn(second_ref[...], c_ref[...]))
-        put(1, every, dot_tn(first_ref[...], ds_ref[...]))
-        put(2, half_of(h), dot_tn(am_ref[...], df))
-        put(2, half_of(1 - h), dot_tn(ao_ref[...], df))
-        put(3, every, dot_tn(f_ref[...], df))
+                df = df_ref[...]
+                out_ref[0, half_of(h), :] = dot_tn(am_ref[...], df).astype(BF)
+                out_ref[0, half_of(1 - h), :] = dot_tn(ao_ref[...], df).astype(BF)
+                out_ref[1] = dot_tn(f_ref[...], df).astype(BF)
+
+        return body
 
     pair_grads = ((2, width, width), BF)
-    keep, send = call(
-        grads_body, [pair_grads, pair_grads],
-        [features, cotangent, agg_mine, agg_other, first, second, delta_second, delta_first],
-        flops=4 * flops,
-    )
+    nodes = [features, cotangent, agg_mine, agg_other, first, second, delta_second, delta_first]
+    send = call(grads_body(True), [pair_grads], nodes, flops=2 * flops)[0]
     got = swap(send, "row", 1)
+    keep = call(grads_body(False), [pair_grads], nodes, flops=2 * flops)[0]
 
     def ends_body(f_ref, c_ref, second_ref, df_ref, wo_ref, ws_ref, up_ref, gs_ref):
         up_ref[...] = (f_ref[...].astype(F32) + dot(second_ref[...], wo_ref[...])).astype(BF)
@@ -284,7 +271,13 @@
     flips = [2 * d for d in range(chips)]
     cut = width // 2
     share = ((reps, share_rows, cut), BF)
-    slab = ((2, level_rows, cut), BF)
+
+    def stack(count):
+        return ((count, 2, level_rows, cut), BF)
+
+    bits = [1 << t for t in range(reps.bit_length() - 1)]
+    kept = [e for e in range(reps) if not e & bits[0]]
+    sent = [e for e in range(reps) if e & bits[0]]
 
     def share_at(number):
         start = lax.rem(number, chips // 2) * share_rows
@@ -302,15 +295,31 @@
                     k_ref[which, here, :cut].astype(F32) + g_ref[which, here, :cut].astype(F32)
                 ).astype(BF)
             here = pl.ds(first, level_rows)
+            side, place = (kept, 0) if e in kept else (sent, 1)
             for i in range(2):
-                outs[chips + e][i] = (
+                outs[chips + place][side.index(e), i] = (
                     k_ref[i, here, cut:].astype(F32) + g_ref[i, here, cut:].astype(F32)
                 ).astype(BF)
 
-    packs = call(pack_body, [share] * chips + [slab] * reps, [keep, got])
+    packs = call(pack_body, [share] * chips + [stack(len(kept)), stack(len(sent))], [keep, got])
     planes = [packs[0]] + [swap(packs[n], "row", flips[n]) for n in range(1, chips)]
-    slabs = packs[chips:]
-    slabs = [slabs[0]] + [swap(slabs[e], "rep", e) for e in range(1, reps)]
+
+    slab_keep = packs[chips]
+    slab_in = swap(packs[chips + 1], "rep", bits[0])
+    for bit in bits[1:]:
+        stay = [n for n, e in enumerate(kept) if not e & bit]
+        leave = [n for n, e in enumerate(kept) if e & bit]
+
+        def halve_body(own_ref, in_ref, stay_ref, leave_ref, stay=stay, leave=leave):
+            for out, numbers in ((stay_ref, stay), (leave_ref, leave)):
+                for n, source in enumerate(numbers):
+                    out[n] = (own_ref[source].astype(F32) + in_ref[source].astype(F32)).astype(BF)
+
+        slab_keep, slab_send = call(
+            halve_body, [stack(len(stay)), stack(len(leave))], [slab_keep, slab_in]
+        )
+        kept = [kept[n] for n in stay]
+        slab_in = swap(slab_send, "rep", bit)
 
     def plane_body(*refs):
         ins, outs = refs[:chips], refs[chips:]
@@ -334,16 +343,13 @@
     gathered = [mine] + [swap(mine, "row", flips[n]) for n in range(1, chips)]
     others = [swap(v, "row", 1) for v in gathered]
 
-    slab_sum = call(level_body, [slab], slabs)[0]
-    spans = [slab_sum] + [swap(slab_sum, "row", flips[n]) for n in range(1, chips)]
-
-    def span_body(*refs):
-        terms = [ref[...].astype(F32) for ref in refs[:-1]]
-        while len(terms) > 1:
-            terms = [a + b for a, b in zip(terms[::2], terms[1::2])]
-        refs[-1][...] = terms[0].astype(BF)
-
-    span = call(span_body, [slab], spans)[0]
+    def span_body(a_ref, b_ref, out_ref):
+        out_ref[...] = (a_ref[...].astype(F32) + b_ref[...].astype(F32)).astype(BF)
+
+    span = call(span_body, [stack(1)], [slab_keep, slab_in])[0]
+    for flip in reversed(span_flips(chips)):
+        moved = swap(span, "row", flip)
+        span = call(span_body, [stack(1)], [span, moved])[0]
     span_other = swap(span, "row", 1)
 
     def out_body(*refs):
@@ -367,7 +373,7 @@
             for i in range(2):
                 put(
                     side * 2 + i, pl.ds(0, level_rows), pl.ds(cut, width - cut),
-                    slab_ref[i].astype(F32) * scale,
+                    slab_ref[0, i].astype(F32) * scale,
                 )
 
     final = ((level_rows, width), F32)

time: 111 us -> 104 us (0.937)
  starting transfers between devices: 55.6 us -> 45.5 us
  waiting for transfers between devices: 39.6 us -> 44.6 us
  local copies, waits for them, and re-layouts: 2.7 us -> 1 us
    ppermute x36 -> x34, starting transfers between devices: 46.7 us -> 35.6 us  [swap(): return lax.ppermute(value, axis, [(i, i ^ flip) for i in range(count)])]
    ppermute x6, waiting for transfers between devices: 3.21 us -> 5.75 us  [swap_off(): return lax.ppermute(value, 'row', pairs)]
    ppermute x36 -> x34, waiting for transfers between devices: 36.4 us -> 38.8 us  [swap(): return lax.ppermute(value, axis, [(i, i ^ flip) for i in range(count)])]
    unnamed x18, local copies, waits for them, and re-layouts: 2.7 us -> 1 us
    pallas_call x20 -> x24, Pallas kernels: 11.5 us -> 11.5 us  [call(): pl.pallas_call(body, out_shape=[jax.ShapeDtypeStruct(shape, dtype) for sh...]
  transfers between devices with their start and end apart: 42 -> 40, of which waited for: 15 -> 16; matrix products, arithmetic and copies ran while one was open for 0% -> 0% of each run, Pallas kernels for 7% -> 8%
where the time goes in v1:
time: 104 us
  starting transfers between devices  45.5 us (44%)
  waiting for transfers between devices  44.6 us (43%)
  Pallas kernels  11.5 us (11%)
    ppermute x34, waiting for transfers between devices, swap(): return lax.ppermute(value, axis, [(i, i ^ flip) for i in range(count)])  38.8 us
    ppermute x34, starting transfers between devices, swap(): return lax.ppermute(value, axis, [(i, i ^ flip) for i in range(count)])  35.6 us
    pallas_call x24, Pallas kernels, call(): pl.pallas_call(body, out_shape=[jax.ShapeDtypeStruct(shape, dtype) for sh...  11.5 us
    ppermute x6, starting transfers between devices, swap_off(): return lax.ppermute(value, 'row', pairs)  9.94 us
    ppermute x6, waiting for transfers between devices, swap_off(): return lax.ppermute(value, 'row', pairs)  5.75 us
  transfers between devices with their start and end apart: 40, of which 16 were waited for; matrix products, arithmetic and copies ran while one was open for 0% of the time, Pallas kernels for 8%

profile of v1, /device:TPU:0, one launch (start us, length us, event | category | flops | bytes accessed | tf_op | source)
XLA Modules:
  0.0 103.6 jit_solution(14043728480353850247)
XLA Ops:
  0.6 3.1 %collective-permute-start.11 = (bf16[2,8,128,128]{3,2,1,0:T(8,128)(2,1)}, bf16[2,8,128,128]{3,2,1,0:T(8,128)(2,1)S(1)}, u32[]{:S(2)}, u32[]{:S(2)}) collective-permute-start(bf16[2,8,128,128]{3,2,1,0:T(8,128)(2,1)} %t_ref.1), channel_id=1, source_target_pairs={{0,1},{1,0},{2,3},{3,2},{4,5},{5,4},{6,7},{7,6},{8,9},{9,8},{10,11... | collective-permute-start | bytes 1572872 | tf_op jit(solution)/shard_map/ppermute | solution.py:19
  3.8 0.9 copy-done
  4.7 2.7 %collective-permute-start.1 = (bf16[256,256]{1,0:T(8,128)(2,1)S(1)}, bf16[256,256]{1,0:T(8,128)(2,1)S(1)}, u32[]{:S(2)}, u32[]{:S(2)}) collective-permute-start(bf16[256,256]{1,0:T(8,128)(2,1)S(1)} %get-tuple-element.45.refs_0_), channel_id=1, source_target_pairs={{0,2},{1,3},{2,0},{3,1},{4,6},{5,7},{6,4},{7,5},{8,10},{9,11},{10,... | collective-permute-start | bytes 393224 | tf_op jit(solution)/shard_map/ppermute | solution.py:19
  7.4 0.9 collective-permute-start.12
  8.3 1.1 %collective-permute-start = (bf16[256,256]{1,0:T(8,128)(2,1)S(1)}, bf16[256,256]{1,0:T(8,128)(2,1)S(1)}, u32[]{:S(2)}, u32[]{:S(2)}) collective-permute-start(bf16[256,256]{1,0:T(8,128)(2,1)S(1)} %get-tuple-element.46), channel_id=1, source_target_pairs={{0,1},{1,0},{2,3},{3,2},{4,5},{5,4},{6,7},{7,6},{8,9},{9,8},{10,11... | collective-permute-start | bytes 393224 | tf_op jit(solution)/shard_map/ppermute | solution.py:19
  9.4 12.5 %collective-permute-done.12.c_ref = s32[2,8]{1,0:T(2,128)S(1)} collective-permute-done((s32[2,8]{1,0:T(2,128)}, s32[2,8]{1,0:T(2,128)S(1)}, u32[]{:S(2)}, u32[]{:S(2)}) %collective-permute-start.12) | collective-permute-done | bytes 96 | tf_op jit(solution)/shard_map/ppermute | solution.py:19
  21.9 2.6 %collective-permute-start.7 = (bf16[256,256]{1,0:T(8,128)(2,1)S(1)}, bf16[256,256]{1,0:T(8,128)(2,1)S(1)}, u32[]{:S(2)}, u32[]{:S(2)}) collective-permute-start(bf16[256,256]{1,0:T(8,128)(2,1)S(1)} %get-tuple-element.45.refs_0_), channel_id=1, source_target_pairs={{0,28},{4,8},{8,4},{12,16},{16,12},{20,24},{24,20},{28,0},{1,29},{... | collective-permute-start | bytes 393224 | tf_op jit(solution)/shard_map/ppermute | solution.py:25
  24.8 2.6 %collective-permute-start.9 = (bf16[256,256]{1,0:T(8,128)(2,1)S(1)}, bf16[256,256]{1,0:T(8,128)(2,1)S(1)}, u32[]{:S(2)}, u32[]{:S(2)}) collective-permute-start(bf16[256,256]{1,0:T(8,128)(2,1)S(1)} %collective-permute-done.1.refs_2_), channel_id=1, source_target_pairs={{0,28},{4,8},{8,4},{12,16},{16,12},{20,24},{24,20},{28,0},{1,29},{... | collective-permute-start | bytes 393224 | tf_op jit(solution)/shard_map/ppermute | solution.py:25
  28.4 2.2 %collective-permute-start.8 = (bf16[256,256]{1,0:T(8,128)(2,1)S(1)}, bf16[256,256]{1,0:T(8,128)(2,1)S(1)}, u32[]{:S(2)}, u32[]{:S(2)}) collective-permute-start(bf16[256,256]{1,0:T(8,128)(2,1)S(1)} %collective-permute-done.refs_1_), channel_id=1, source_target_pairs={{0,28},{4,8},{8,4},{12,16},{16,12},{20,24},{24,20},{28,0},{1,29},{... | collective-permute-start | bytes 393224 | tf_op jit(solution)/shard_map/ppermute | solution.py:25
  30.6 0.9 shard_map.130.a_ref
  31.5 2.5 %collective-permute-done.10.refs_11_ = bf16[256,256]{1,0:T(8,128)(2,1)S(1)} collective-permute-done((bf16[256,256]{1,0:T(8,128)(2,1)S(1)}, bf16[256,256]{1,0:T(8,128)(2,1)S(1)}, u32[]{:S(2)}, u32[]{:S(2)}) %collective-permute-start.10) | collective-permute-done | bytes 131104 | tf_op jit(solution)/shard_map/ppermute | solution.py:25
  34.1 2.8 %collective-permute-done.8.refs_9_ = bf16[256,256]{1,0:T(8,128)(2,1)S(1)} collective-permute-done((bf16[256,256]{1,0:T(8,128)(2,1)S(1)}, bf16[256,256]{1,0:T(8,128)(2,1)S(1)}, u32[]{:S(2)}, u32[]{:S(2)}) %collective-permute-start.8) | collective-permute-done | bytes 131104 | tf_op jit(solution)/shard_map/ppermute | solution.py:25
  36.9 0.6 shard_map.131
  37.5 2.5 %collective-permute-start.13 = (bf16[256,256]{1,0:T(8,128)(2,1)S(1)}, bf16[256,256]{1,0:T(8,128)(2,1)S(1)}, u32[]{:S(2)}, u32[]{:S(2)}) collective-permute-start(bf16[256,256]{1,0:T(8,128)(2,1)S(1)} %shard_map.131), channel_id=1, source_target_pairs={{0,1},{1,0},{2,3},{3,2},{4,5},{5,4},{6,7},{7,6},{8,9},{9,8},{10,11... | collective-permute-start | bytes 393224 | tf_op jit(solution)/shard_map/ppermute | solution.py:19
  40.0 1.2 %shard_map.127 = (bf16[24,256,128]{2,1,0:T(8,128)(2,1)S(1)}, bf16[24,128,256]{2,1,0:T(8,128)(2,1)S(1)}) custom-call(bf16[2,8,128,128]{3,2,1,0:T(8,128)(2,1)S(1)} %copy-done.5, s32[2,8]{1,0:T(2,128)S(1)} %copy-done.8), custom_call_target="tpu_custom_call" | custom-call | bytes 3670080 | tf_op jit(solution)/shard_map/pallas_call | solution.py:38
  41.7 0.6 shard_map.129.am_ref
  42.3 1.2 %collective-permute-done.13.ao_ref = bf16[256,256]{1,0:T(8,128)(2,1)S(1)} collective-permute-done((bf16[256,256]{1,0:T(8,128)(2,1)S(1)}, bf16[256,256]{1,0:T(8,128)(2,1)S(1)}, u32[]{:S(2)}, u32[]{:S(2)}) %collective-permute-start.13) | collective-permute-done | bytes 131104 | tf_op jit(solution)/shard_map/ppermute | solution.py:19
  43.5 1.1 %shard_map.133 = (bf16[256,256]{1,0:T(8,128)(2,1)S(1)}, bf16[256,256]{1,0:T(8,128)(2,1)S(1)}, bf16[256,512]{1,0:T(8,128)(2,1)S(1)}, bf16[256,512]{1,0:T(8,128)(2...) custom-call(bf16[256,256]{1,0:T(8,128)(2,1)S(1)} %shard_map.129.am_ref, ...), custom_call_target="tpu_custom_call" | custom-call | flops 536870912 | bytes 3670016 | tf_op jit(solution)/shard_map/pallas_call | solution.py:38
  45.1 1.8 %collective-permute-start.14 = (bf16[256,256]{1,0:T(8,128)(2,1)S(1)}, bf16[256,256]{1,0:T(8,128)(2,1)S(1)}, u32[]{:S(2)}, u32[]{:S(2)}) collective-permute-start(bf16[256,256]{1,0:T(8,128)(2,1)S(1)} %get-tuple-element.55), channel_id=1, source_target_pairs={{0,1},{1,0},{2,3},{3,2},{4,5},{5,4},{6,7},{7,6},{8,9},{9,8},{10,11... | collective-permute-start | bytes 393224 | tf_op jit(solution)/shard_map/ppermute | solution.py:19
  46.9 0.8 shard_map.135.ap_ref
  48.6 1.3 %collective-permute-start.35 = (bf16[2,2,128,256]{3,2,1,0:T(8,128)(2,1)S(1)}, bf16[2,2,128,256]{3,2,1,0:T(8,128)(2,1)S(1)}, u32[]{:S(2)}, u32[]{:S(2)}) collective-permute-start(bf16[2,2,128,256]{3,2,1,0:T(8,128)(2,1)S(1)} %get-tuple-element.75), channel_id=1, source_target_pairs={{0,1},{1,0},{2,3},{3,2},{4,5},{5,4},{6,7},{7,6},{8,9},{9,8},{10,11... | collective-permute-start | bytes 786440 | tf_op jit(solution)/shard_map/ppermute | solution.py:19
  49.8 1.2 %collective-permute-done.14.dp_ref = bf16[256,256]{1,0:T(8,128)(2,1)S(1)} collective-permute-done((bf16[256,256]{1,0:T(8,128)(2,1)S(1)}, bf16[256,256]{1,0:T(8,128)(2,1)S(1)}, u32[]{:S(2)}, u32[]{:S(2)}) %collective-permute-start.14) | collective-permute-done | bytes 131104 | tf_op jit(solution)/shard_map/ppermute | solution.py:19
  51.0 0.7 shard_map.136
  52.3 2.1 %collective-permute-start.18 = (bf16[512,256]{1,0:T(8,128)(2,1)S(1)}, bf16[512,256]{1,0:T(8,128)(2,1)S(1)}, u32[]{:S(2)}, u32[]{:S(2)}) collective-permute-start(bf16[512,256]{1,0:T(8,128)(2,1)S(1)} %get-tuple-element.61), channel_id=1, source_target_pairs={{0,28},{4,8},{8,4},{12,16},{16,12},{20,24},{24,20},{28,0},{1,29},{... | collective-permute-start | bytes 786440 | tf_op jit(solution)/shard_map/ppermute | solution.py:25
  54.3 2.7 %collective-permute-done.35.in_ref = bf16[2,2,128,256]{3,2,1,0:T(8,128)(2,1)S(1)} collective-permute-done((bf16[2,2,128,256]{3,2,1,0:T(8,128)(2,1)S(1)}, bf16[2,2,128,256]{3,2,1,0:T(8,128)(2,1)S(1)}, u32[]{:S(2)}, u32[]{:S(2)}) %collective-permute-start.35) | collective-permute-done | bytes 262176 | tf_op jit(solution)/shard_map/ppermute | solution.py:19
  57.0 2.7 %collective-permute-start.36 = (bf16[1,2,128,256]{3,2,1,0:T(8,128)(2,1)S(1)}, bf16[1,2,128,256]{3,2,1,0:T(8,128)(2,1)S(1)}, u32[]{:S(2)}, u32[]{:S(2)}) collective-permute-start(bf16[1,2,128,256]{3,2,1,0:T(8,128)(2,1)S(1)} %get-tuple-element.77), channel_id=1, source_target_pairs={{0,2},{1,3},{2,0},{3,1},{4,6},{5,7},{6,4},{7,5},{8,10},{9,11},{10,... | collective-permute-start | bytes 393224 | tf_op jit(solution)/shard_map/ppermute | solution.py:19
  60.2 5.3 %collective-permute-done.36.b_ref = bf16[1,2,128,256]{3,2,1,0:T(8,128)(2,1)S(1)} collective-permute-done((bf16[1,2,128,256]{3,2,1,0:T(8,128)(2,1)S(1)}, bf16[1,2,128,256]{3,2,1,0:T(8,128)(2,1)S(1)}, u32[]{:S(2)}, u32[]{:S(2)}) %collective-permute-start.36) | collective-permute-done | bytes 131104 | tf_op jit(solution)/shard_map/ppermute | solution.py:19
  65.5 1.2 %collective-permute-start.37 = (bf16[1,2,128,256]{3,2,1,0:T(8,128)(2,1)S(1)}, bf16[1,2,128,256]{3,2,1,0:T(8,128)(2,1)S(1)}, u32[]{:S(2)}, u32[]{:S(2)}) collective-permute-start(bf16[1,2,128,256]{3,2,1,0:T(8,128)(2,1)S(1)} %shard_map.147.a_ref), channel_id=1, source_target_pairs={{0,16},{4,20},{8,24},{12,28},{16,0},{20,4},{24,8},{28,12},{1,17},{... | collective-permute-start | bytes 393224 | tf_op jit(solution)/shard_map/ppermute | solution.py:19
  66.8 1.3 %collective-permute-start.22 = (bf16[4,64,256]{2,1,0:T(8,128)(2,1)S(1)}, bf16[4,64,256]{2,1,0:T(8,128)(2,1)S(1)}, u32[]{:S(2)}, u32[]{:S(2)}) collective-permute-start(bf16[4,64,256]{2,1,0:T(8,128)(2,1)S(1)} %get-tuple-element.67), channel_id=1, source_target_pairs={{0,8},{4,12},{8,0},{12,4},{16,24},{20,28},{24,16},{28,20},{1,9},{5... | collective-permute-start | bytes 393224 | tf_op jit(solution)/shard_map/ppermute | solution.py:19
  68.2 3.8 %collective-permute-done.37.b_ref = bf16[1,2,128,256]{3,2,1,0:T(8,128)(2,1)S(1)} collective-permute-done((bf16[1,2,128,256]{3,2,1,0:T(8,128)(2,1)S(1)}, bf16[1,2,128,256]{3,2,1,0:T(8,128)(2,1)S(1)}, u32[]{:S(2)}, u32[]{:S(2)}) %collective-permute-start.37) | collective-permute-done | bytes 131104 | tf_op jit(solution)/shard_map/ppermute | solution.py:19
  72.0 1.6 %collective-permute-start.24 = (bf16[4,64,256]{2,1,0:T(8,128)(2,1)S(1)}, bf16[4,64,256]{2,1,0:T(8,128)(2,1)S(1)}, u32[]{:S(2)}, u32[]{:S(2)}) collective-permute-start(bf16[4,64,256]{2,1,0:T(8,128)(2,1)S(1)} %get-tuple-element.69), channel_id=1, source_target_pairs={{0,24},{4,28},{8,16},{12,20},{16,8},{20,12},{24,0},{28,4},{1,25},{... | collective-permute-start | bytes 393224 | tf_op jit(solution)/shard_map/ppermute | solution.py:19
  73.6 1.1 %collective-permute-start.38 = (bf16[1,2,128,256]{3,2,1,0:T(8,128)(2,1)S(1)}, bf16[1,2,128,256]{3,2,1,0:T(8,128)(2,1)S(1)}, u32[]{:S(2)}, u32[]{:S(2)}) collective-permute-start(bf16[1,2,128,256]{3,2,1,0:T(8,128)(2,1)S(1)} %shard_map.148.a_ref), channel_id=1, source_target_pairs={{0,8},{4,12},{8,0},{12,4},{16,24},{20,28},{24,16},{28,20},{1,9},{5... | collective-permute-start | bytes 393224 | tf_op jit(solution)/shard_map/ppermute | solution.py:19
  74.8 0.6 collective-permute-start.19
  75.4 3.1 %collective-permute-start.20 = (bf16[256,256]{1,0:T(8,128)(2,1)S(1)}, bf16[256,256]{1,0:T(8,128)(2,1)S(1)}, u32[]{:S(2)}, u32[]{:S(2)}) collective-permute-start(bf16[256,256]{1,0:T(8,128)(2,1)S(1)} %get-tuple-element.63), channel_id=1, source_target_pairs={{0,3},{1,2},{2,1},{3,0},{4,7},{5,6},{6,5},{7,4},{8,11},{9,10},{10,... | collective-permute-start | bytes 393224 | tf_op jit(solution)/shard_map/ppermute | solution.py:19
  79.2 1.6 %collective-permute-start.25 = (bf16[64,256]{1,0:T(8,128)(2,1)S(1)}, bf16[64,256]{1,0:T(8,128)(2,1)S(1)}, u32[]{:S(2)}, u32[]{:S(2)}) collective-permute-start(bf16[64,256]{1,0:T(8,128)(2,1)S(1)} %get-tuple-element.71), channel_id=1, source_target_pairs={{0,1},{1,0},{2,3},{3,2},{4,5},{5,4},{6,7},{7,6},{8,9},{9,8},{10,11... | collective-permute-start | bytes 98312 | tf_op jit(solution)/shard_map/ppermute | solution.py:19
  80.9 1.9 %collective-permute-start.26 = (bf16[64,256]{1,0:T(8,128)(2,1)S(1)}, bf16[64,256]{1,0:T(8,128)(2,1)S(1)}, u32[]{:S(2)}, u32[]{:S(2)}) collective-permute-start(bf16[64,256]{1,0:T(8,128)(2,1)S(1)} %get-tuple-element.72), channel_id=1, source_target_pairs={{0,2},{1,3},{2,0},{3,1},{4,6},{5,7},{6,4},{7,5},{8,10},{9,11},{10,... | collective-permute-start | bytes 98312 | tf_op jit(solution)/shard_map/ppermute | solution.py:19
  82.8 3.9 %collective-permute-done.25.refs_1_ = bf16[64,256]{1,0:T(8,128)(2,1)S(1)} collective-permute-done((bf16[64,256]{1,0:T(8,128)(2,1)S(1)}, bf16[64,256]{1,0:T(8,128)(2,1)S(1)}, u32[]{:S(2)}, u32[]{:S(2)}) %collective-permute-start.25) | collective-permute-done | bytes 32800 | tf_op jit(solution)/shard_map/ppermute | solution.py:19
  86.8 1.7 %collective-permute-done.26.refs_2_ = bf16[64,256]{1,0:T(8,128)(2,1)S(1)} collective-permute-done((bf16[64,256]{1,0:T(8,128)(2,1)S(1)}, bf16[64,256]{1,0:T(8,128)(2,1)S(1)}, u32[]{:S(2)}, u32[]{:S(2)}) %collective-permute-start.26) | collective-permute-done | bytes 32800 | tf_op jit(solution)/shard_map/ppermute | solution.py:19
  88.4 2.1 %collective-permute-start.27 = (bf16[64,256]{1,0:T(8,128)(2,1)S(1)}, bf16[64,256]{1,0:T(8,128)(2,1)S(1)}, u32[]{:S(2)}, u32[]{:S(2)}) collective-permute-start(bf16[64,256]{1,0:T(8,128)(2,1)S(1)} %get-tuple-element.73), channel_id=1, source_target_pairs={{0,3},{1,2},{2,1},{3,0},{4,7},{5,6},{6,5},{7,4},{8,11},{9,10},{10,... | collective-permute-start | bytes 98312 | tf_op jit(solution)/shard_map/ppermute | solution.py:19
  90.6 3.6 %collective-permute-done.27.refs_3_ = bf16[64,256]{1,0:T(8,128)(2,1)S(1)} collective-permute-done((bf16[64,256]{1,0:T(8,128)(2,1)S(1)}, bf16[64,256]{1,0:T(8,128)(2,1)S(1)}, u32[]{:S(2)}, u32[]{:S(2)}) %collective-permute-start.27) | collective-permute-done | bytes 32800 | tf_op jit(solution)/shard_map/ppermute | solution.py:19
  94.2 0.8 collective-permute-start.28
  95.0 0.6 collective-permute-start.29
  95.6 2.1 %collective-permute-start.30 = (bf16[64,256]{1,0:T(8,128)(2,1)S(1)}, bf16[64,256]{1,0:T(8,128)(2,1)S(1)}, u32[]{:S(2)}, u32[]{:S(2)}) collective-permute-start(bf16[64,256]{1,0:T(8,128)(2,1)S(1)} %shard_map.145.refs_0_), channel_id=1, source_target_pairs={{0,24},{4,28},{8,16},{12,20},{16,8},{20,12},{24,0},{28,4},{1,25},{... | collective-permute-start | bytes 98312 | tf_op jit(solution)/shard_map/ppermute | solution.py:19
  98.3 0.7 collective-permute-done.29.refs_2_
  98.9 1.5 %collective-permute-done.30.refs_3_ = bf16[64,256]{1,0:T(8,128)(2,1)S(1)} collective-permute-done((bf16[64,256]{1,0:T(8,128)(2,1)S(1)}, bf16[64,256]{1,0:T(8,128)(2,1)S(1)}, u32[]{:S(2)}, u32[]{:S(2)}) %collective-permute-start.30) | collective-permute-done | bytes 32800 | tf_op jit(solution)/shard_map/ppermute | solution.py:19
  100.4 1.0 shard_map.134
  101.4 0.8 shard_map.140
  102.2 1.3 %shard_map.150 = (f32[128,512]{1,0:T(8,128)}, f32[128,512]{1,0:T(8,128)}, f32[128,512]{1,0:T(8,128)}, f32[128,512]{1,0:T(8,128)}) custom-call(bf16[64,256]{1,0:T(8,128)(2,1)S(1)} %shard_map.145.refs_0_, bf16[64,256]{1,0:T(8,128)(2,1)S(1)} %collective-permute-done.28.refs_1_, bf16[64,256]{1,0:T(8,128)(2,1)S(1)} %collective-permute-done.29.refs_2_, ...), custom_call_target="tpu_custom_call" | custom-call | bytes 1572864 | tf_op jit(solution)/shard_map/pallas_call | solution.py:38
  (74 shorter events, 5.8 us)
Async XLA Ops:
  0.6 27.8 %collective-permute-start.11 = (bf16[2,8,128,128]{3,2,1,0:T(8,128)(2,1)}, bf16[2,8,128,128]{3,2,1,0:T(8,128)(2,1)S(1)}, u32[]{:S(2)}, u32[]{:S(2)}) collective-permute-start(bf16[2,8,128,128]{3,2,1,0:T(8,128)(2,1)} %t_ref.1), channel_id=1, source_target_pairs={{0,1},{1,0},{2,3},{3,2},{4,5},{5,4},{6,7},{7,6},{8,9},{9,8},{10,11... | collective-permute-start | bytes 1572872 | tf_op jit(solution)/shard_map/ppermute | solution.py:19
  4.7 17.2 %collective-permute-start.1 = (bf16[256,256]{1,0:T(8,128)(2,1)S(1)}, bf16[256,256]{1,0:T(8,128)(2,1)S(1)}, u32[]{:S(2)}, u32[]{:S(2)}) collective-permute-start(bf16[256,256]{1,0:T(8,128)(2,1)S(1)} %get-tuple-element.45.refs_0_), channel_id=1, source_target_pairs={{0,2},{1,3},{2,0},{3,1},{4,6},{5,7},{6,4},{7,5},{8,10},{9,11},{10,... | collective-permute-start | bytes 393224 | tf_op jit(solution)/shard_map/ppermute | solution.py:19
  7.4 17.4 %collective-permute-start.2 = (bf16[256,256]{1,0:T(8,128)(2,1)S(1)}, bf16[256,256]{1,0:T(8,128)(2,1)S(1)}, u32[]{:S(2)}, u32[]{:S(2)}) collective-permute-start(bf16[256,256]{1,0:T(8,128)(2,1)S(1)} %get-tuple-element.46), channel_id=1, source_target_pairs={{0,3},{1,2},{2,1},{3,0},{4,7},{5,6},{6,5},{7,4},{8,11},{9,10},{10,... | collective-permute-start | bytes 393224 | tf_op jit(solution)/shard_map/ppermute | solution.py:19
  7.4 14.5 %collective-permute-start.12 = (s32[2,8]{1,0:T(2,128)}, s32[2,8]{1,0:T(2,128)S(1)}, u32[]{:S(2)}, u32[]{:S(2)}) collective-permute-start(s32[2,8]{1,0:T(2,128)} %c_ref.5), channel_id=1, source_target_pairs={{0,1},{1,0},{2,3},{3,2},{4,5},{5,4},{6,7},{7,6},{8,9},{9,8},{10,11... | collective-permute-start | bytes 200 | tf_op jit(solution)/shard_map/ppermute | solution.py:19
  8.3 16.6 %collective-permute-start = (bf16[256,256]{1,0:T(8,128)(2,1)S(1)}, bf16[256,256]{1,0:T(8,128)(2,1)S(1)}, u32[]{:S(2)}, u32[]{:S(2)}) collective-permute-start(bf16[256,256]{1,0:T(8,128)(2,1)S(1)} %get-tuple-element.46), channel_id=1, source_target_pairs={{0,1},{1,0},{2,3},{3,2},{4,5},{5,4},{6,7},{7,6},{8,9},{9,8},{10,11... | collective-permute-start | bytes 393224 | tf_op jit(solution)/shard_map/ppermute | solution.py:19
  21.9 5.5 %collective-permute-start.3 = (bf16[256,256]{1,0:T(8,128)(2,1)S(1)}, bf16[256,256]{1,0:T(8,128)(2,1)S(1)}, u32[]{:S(2)}, u32[]{:S(2)}) collective-permute-start(bf16[256,256]{1,0:T(8,128)(2,1)S(1)} %get-tuple-element.45.refs_0_), channel_id=1, source_target_pairs={{0,4},{4,0},{8,12},{12,8},{16,20},{20,16},{24,28},{28,24},{1,5},{5... | collective-permute-start | bytes 393224 | tf_op jit(solution)/shard_map/ppermute | solution.py:19
  21.9 6.0 %collective-permute-start.7 = (bf16[256,256]{1,0:T(8,128)(2,1)S(1)}, bf16[256,256]{1,0:T(8,128)(2,1)S(1)}, u32[]{:S(2)}, u32[]{:S(2)}) collective-permute-start(bf16[256,256]{1,0:T(8,128)(2,1)S(1)} %get-tuple-element.45.refs_0_), channel_id=1, source_target_pairs={{0,28},{4,8},{8,4},{12,16},{16,12},{20,24},{24,20},{28,0},{1,29},{... | collective-permute-start | bytes 393224 | tf_op jit(solution)/shard_map/ppermute | solution.py:25
  24.8 3.2 %collective-permute-start.5 = (bf16[256,256]{1,0:T(8,128)(2,1)S(1)}, bf16[256,256]{1,0:T(8,128)(2,1)S(1)}, u32[]{:S(2)}, u32[]{:S(2)}) collective-permute-start(bf16[256,256]{1,0:T(8,128)(2,1)S(1)} %collective-permute-done.1.refs_2_), channel_id=1, source_target_pairs={{0,4},{4,0},{8,12},{12,8},{16,20},{20,16},{24,28},{28,24},{1,5},{5... | collective-permute-start | bytes 393224 | tf_op jit(solution)/shard_map/ppermute | solution.py:19
  24.8 6.7 %collective-permute-start.9 = (bf16[256,256]{1,0:T(8,128)(2,1)S(1)}, bf16[256,256]{1,0:T(8,128)(2,1)S(1)}, u32[]{:S(2)}, u32[]{:S(2)}) collective-permute-start(bf16[256,256]{1,0:T(8,128)(2,1)S(1)} %collective-permute-done.1.refs_2_), channel_id=1, source_target_pairs={{0,28},{4,8},{8,4},{12,16},{16,12},{20,24},{24,20},{28,0},{1,29},{... | collective-permute-start | bytes 393224 | tf_op jit(solution)/shard_map/ppermute | solution.py:25
  27.4 6.7 %collective-permute-start.10 = (bf16[256,256]{1,0:T(8,128)(2,1)S(1)}, bf16[256,256]{1,0:T(8,128)(2,1)S(1)}, u32[]{:S(2)}, u32[]{:S(2)}) collective-permute-start(bf16[256,256]{1,0:T(8,128)(2,1)S(1)} %collective-permute-done.2.refs_3_), channel_id=1, source_target_pairs={{0,28},{4,8},{8,4},{12,16},{16,12},{20,24},{24,20},{28,0},{1,29},{... | collective-permute-start | bytes 393224 | tf_op jit(solution)/shard_map/ppermute | solution.py:25
  27.9 6.2 %collective-permute-start.6 = (bf16[256,256]{1,0:T(8,128)(2,1)S(1)}, bf16[256,256]{1,0:T(8,128)(2,1)S(1)}, u32[]{:S(2)}, u32[]{:S(2)}) collective-permute-start(bf16[256,256]{1,0:T(8,128)(2,1)S(1)} %collective-permute-done.2.refs_3_), channel_id=1, source_target_pairs={{0,4},{4,0},{8,12},{12,8},{16,20},{20,16},{24,28},{28,24},{1,5},{5... | collective-permute-start | bytes 393224 | tf_op jit(solution)/shard_map/ppermute | solution.py:19
  28.0 6.1 %collective-permute-start.4 = (bf16[256,256]{1,0:T(8,128)(2,1)S(1)}, bf16[256,256]{1,0:T(8,128)(2,1)S(1)}, u32[]{:S(2)}, u32[]{:S(2)}) collective-permute-start(bf16[256,256]{1,0:T(8,128)(2,1)S(1)} %collective-permute-done.refs_1_), channel_id=1, source_target_pairs={{0,4},{4,0},{8,12},{12,8},{16,20},{20,16},{24,28},{28,24},{1,5},{5... | collective-permute-start | bytes 393224 | tf_op jit(solution)/shard_map/ppermute | solution.py:19
  28.4 8.5 %collective-permute-start.8 = (bf16[256,256]{1,0:T(8,128)(2,1)S(1)}, bf16[256,256]{1,0:T(8,128)(2,1)S(1)}, u32[]{:S(2)}, u32[]{:S(2)}) collective-permute-start(bf16[256,256]{1,0:T(8,128)(2,1)S(1)} %collective-permute-done.refs_1_), channel_id=1, source_target_pairs={{0,28},{4,8},{8,4},{12,16},{16,12},{20,24},{24,20},{28,0},{1,29},{... | collective-permute-start | bytes 393224 | tf_op jit(solution)/shard_map/ppermute | solution.py:25
  31.5 8.5 %copy-start.5 = (bf16[2,8,128,128]{3,2,1,0:T(8,128)(2,1)S(1)}, bf16[2,8,128,128]{3,2,1,0:T(8,128)(2,1)}, u32[]{:S(2)}) copy-start(bf16[2,8,128,128]{3,2,1,0:T(8,128)(2,1)} %t_ref.1) | copy-start | bytes 1572868
  31.5 8.5 %copy-start.8 = (s32[2,8]{1,0:T(2,128)S(1)}, s32[2,8]{1,0:T(2,128)}, u32[]{:S(2)}) copy-start(s32[2,8]{1,0:T(2,128)} %c_ref.5) | copy-start | bytes 196
  31.5 9.7 %copy-start.1 = (bf16[256,512]{1,0:T(8,128)(2,1)S(1)}, bf16[256,512]{1,0:T(8,128)(2,1)}, u32[]{:S(2)}) copy-start(bf16[256,512]{1,0:T(8,128)(2,1)} %f_ref.9) | copy-start | bytes 786436
  31.5 9.7 %copy-start.2 = (bf16[256,512]{1,0:T(8,128)(2,1)S(1)}, bf16[256,512]{1,0:T(8,128)(2,1)}, u32[]{:S(2)}) copy-start(bf16[256,512]{1,0:T(8,128)(2,1)} %c_ref.9) | copy-start | bytes 786436
  31.5 9.7 %copy-start.3 = (bf16[512,512]{1,0:T(8,128)(2,1)S(1)}, bf16[512,512]{1,0:T(8,128)(2,1)}, u32[]{:S(2)}) copy-start(bf16[512,512]{1,0:T(8,128)(2,1)} %ws_ref.3) | copy-start | bytes 1572868
  31.5 9.7 %copy-start.4 = (bf16[512,512]{1,0:T(8,128)(2,1)S(1)}, bf16[512,512]{1,0:T(8,128)(2,1)}, u32[]{:S(2)}) copy-start(bf16[512,512]{1,0:T(8,128)(2,1)} %wo_ref.3) | copy-start | bytes 1572868
  37.5 6.0 %collective-permute-start.13 = (bf16[256,256]{1,0:T(8,128)(2,1)S(1)}, bf16[256,256]{1,0:T(8,128)(2,1)S(1)}, u32[]{:S(2)}, u32[]{:S(2)}) collective-permute-start(bf16[256,256]{1,0:T(8,128)(2,1)S(1)} %shard_map.131), channel_id=1, source_target_pairs={{0,1},{1,0},{2,3},{3,2},{4,5},{5,4},{6,7},{7,6},{8,9},{9,8},{10,11... | collective-permute-start | bytes 393224 | tf_op jit(solution)/shard_map/ppermute | solution.py:19
  41.7 1.8 %copy-start.6 = (bf16[512,512]{1,0:T(8,128)(2,1)S(1)}, bf16[512,512]{1,0:T(8,128)(2,1)}, u32[]{:S(2)}) copy-start(bf16[512,512]{1,0:T(8,128)(2,1)} %wa_ref.1) | copy-start | bytes 1572868
  41.7 1.8 %copy-start.7 = (bf16[512,512]{1,0:T(8,128)(2,1)S(1)}, bf16[512,512]{1,0:T(8,128)(2,1)}, u32[]{:S(2)}) copy-start(bf16[512,512]{1,0:T(8,128)(2,1)} %wm_ref.1) | copy-start | bytes 1572868
  45.1 3.2 %collective-permute-start.21 = (bf16[2,512,512]{2,1,0:T(8,128)(2,1)S(1)}, bf16[2,512,512]{2,1,0:T(8,128)(2,1)S(1)}, u32[]{:S(2)}, u32[]{:S(2)}) collective-permute-start(bf16[2,512,512]{2,1,0:T(8,128)(2,1)S(1)} %shard_map.142), channel_id=1, source_target_pairs={{0,4},{4,0},{8,12},{12,8},{16,20},{20,16},{24,28},{28,24},{1,5},{5... | collective-permute-start | bytes 3145736 | tf_op jit(solution)/shard_map/ppermute | solution.py:19
  45.1 5.9 %collective-permute-start.14 = (bf16[256,256]{1,0:T(8,128)(2,1)S(1)}, bf16[256,256]{1,0:T(8,128)(2,1)S(1)}, u32[]{:S(2)}, u32[]{:S(2)}) collective-permute-start(bf16[256,256]{1,0:T(8,128)(2,1)S(1)} %get-tuple-element.55), channel_id=1, source_target_pairs={{0,1},{1,0},{2,3},{3,2},{4,5},{5,4},{6,7},{7,6},{8,9},{9,8},{10,11... | collective-permute-start | bytes 393224 | tf_op jit(solution)/shard_map/ppermute | solution.py:19
  48.6 8.4 %collective-permute-start.35 = (bf16[2,2,128,256]{3,2,1,0:T(8,128)(2,1)S(1)}, bf16[2,2,128,256]{3,2,1,0:T(8,128)(2,1)S(1)}, u32[]{:S(2)}, u32[]{:S(2)}) collective-permute-start(bf16[2,2,128,256]{3,2,1,0:T(8,128)(2,1)S(1)} %get-tuple-element.75), channel_id=1, source_target_pairs={{0,1},{1,0},{2,3},{3,2},{4,5},{5,4},{6,7},{7,6},{8,9},{9,8},{10,11... | collective-permute-start | bytes 786440 | tf_op jit(solution)/shard_map/ppermute | solution.py:19
  51.8 21.9 %collective-permute-start.15 = (bf16[1024,256]{1,0:T(8,128)(2,1)S(1)}, bf16[1024,256]{1,0:T(8,128)(2,1)S(1)}, u32[]{:S(2)}, u32[]{:S(2)}) collective-permute-start(bf16[1024,256]{1,0:T(8,128)(2,1)S(1)} %get-tuple-element.57), channel_id=1, source_target_pairs={{0,4},{4,0},{8,12},{12,8},{16,20},{20,16},{24,28},{28,24},{1,5},{5... | collective-permute-start | bytes 1572872 | tf_op jit(solution)/shard_map/ppermute | solution.py:19
  52.3 15.8 %collective-permute-start.18 = (bf16[512,256]{1,0:T(8,128)(2,1)S(1)}, bf16[512,256]{1,0:T(8,128)(2,1)S(1)}, u32[]{:S(2)}, u32[]{:S(2)}) collective-permute-start(bf16[512,256]{1,0:T(8,128)(2,1)S(1)} %get-tuple-element.61), channel_id=1, source_target_pairs={{0,28},{4,8},{8,4},{12,16},{16,12},{20,24},{24,20},{28,0},{1,29},{... | collective-permute-start | bytes 786440 | tf_op jit(solution)/shard_map/ppermute | solution.py:25
  57.0 8.5 %collective-permute-start.36 = (bf16[1,2,128,256]{3,2,1,0:T(8,128)(2,1)S(1)}, bf16[1,2,128,256]{3,2,1,0:T(8,128)(2,1)S(1)}, u32[]{:S(2)}, u32[]{:S(2)}) collective-permute-start(bf16[1,2,128,256]{3,2,1,0:T(8,128)(2,1)S(1)} %get-tuple-element.77), channel_id=1, source_target_pairs={{0,2},{1,3},{2,0},{3,1},{4,6},{5,7},{6,4},{7,5},{8,10},{9,11},{10,... | collective-permute-start | bytes 393224 | tf_op jit(solution)/shard_map/ppermute | solution.py:19
  59.7 15.1 %collective-permute-start.16 = (bf16[512,256]{1,0:T(8,128)(2,1)S(1)}, bf16[512,256]{1,0:T(8,128)(2,1)S(1)}, u32[]{:S(2)}, u32[]{:S(2)}) collective-permute-start(bf16[512,256]{1,0:T(8,128)(2,1)S(1)} %get-tuple-element.58), channel_id=1, source_target_pairs={{0,28},{4,8},{8,4},{12,16},{16,12},{20,24},{24,20},{28,0},{1,29},{... | collective-permute-start | bytes 786440 | tf_op jit(solution)/shard_map/ppermute | solution.py:25
  65.5 6.4 %collective-permute-start.37 = (bf16[1,2,128,256]{3,2,1,0:T(8,128)(2,1)S(1)}, bf16[1,2,128,256]{3,2,1,0:T(8,128)(2,1)S(1)}, u32[]{:S(2)}, u32[]{:S(2)}) collective-permute-start(bf16[1,2,128,256]{3,2,1,0:T(8,128)(2,1)S(1)} %shard_map.147.a_ref), channel_id=1, source_target_pairs={{0,16},{4,20},{8,24},{12,28},{16,0},{20,4},{24,8},{28,12},{1,17},{... | collective-permute-start | bytes 393224 | tf_op jit(solution)/shard_map/ppermute | solution.py:19
  66.8 8.6 %collective-permute-start.22 = (bf16[4,64,256]{2,1,0:T(8,128)(2,1)S(1)}, bf16[4,64,256]{2,1,0:T(8,128)(2,1)S(1)}, u32[]{:S(2)}, u32[]{:S(2)}) collective-permute-start(bf16[4,64,256]{2,1,0:T(8,128)(2,1)S(1)} %get-tuple-element.67), channel_id=1, source_target_pairs={{0,8},{4,12},{8,0},{12,4},{16,24},{20,28},{24,16},{28,20},{1,9},{5... | collective-permute-start | bytes 393224 | tf_op jit(solution)/shard_map/ppermute | solution.py:19
  68.1 10.5 %collective-permute-start.23 = (bf16[4,64,256]{2,1,0:T(8,128)(2,1)S(1)}, bf16[4,64,256]{2,1,0:T(8,128)(2,1)S(1)}, u32[]{:S(2)}, u32[]{:S(2)}) collective-permute-start(bf16[4,64,256]{2,1,0:T(8,128)(2,1)S(1)} %get-tuple-element.68), channel_id=1, source_target_pairs={{0,16},{4,20},{8,24},{12,28},{16,0},{20,4},{24,8},{28,12},{1,17},{... | collective-permute-start | bytes 393224 | tf_op jit(solution)/shard_map/ppermute | solution.py:19
  72.0 7.2 %collective-permute-start.24 = (bf16[4,64,256]{2,1,0:T(8,128)(2,1)S(1)}, bf16[4,64,256]{2,1,0:T(8,128)(2,1)S(1)}, u32[]{:S(2)}, u32[]{:S(2)}) collective-permute-start(bf16[4,64,256]{2,1,0:T(8,128)(2,1)S(1)} %get-tuple-element.69), channel_id=1, source_target_pairs={{0,24},{4,28},{8,16},{12,20},{16,8},{20,12},{24,0},{28,4},{1,25},{... | collective-permute-start | bytes 393224 | tf_op jit(solution)/shard_map/ppermute | solution.py:19
  73.6 7.2 %collective-permute-start.38 = (bf16[1,2,128,256]{3,2,1,0:T(8,128)(2,1)S(1)}, bf16[1,2,128,256]{3,2,1,0:T(8,128)(2,1)S(1)}, u32[]{:S(2)}, u32[]{:S(2)}) collective-permute-start(bf16[1,2,128,256]{3,2,1,0:T(8,128)(2,1)S(1)} %shard_map.148.a_ref), channel_id=1, source_target_pairs={{0,8},{4,12},{8,0},{12,4},{16,24},{20,28},{24,16},{28,20},{1,9},{5... | collective-permute-start | bytes 393224 | tf_op jit(solution)/shard_map/ppermute | solution.py:19
  74.8 20.2 %collective-permute-start.19 = (bf16[256,256]{1,0:T(8,128)(2,1)S(1)}, bf16[256,256]{1,0:T(8,128)(2,1)S(1)}, u32[]{:S(2)}, u32[]{:S(2)}) collective-permute-start(bf16[256,256]{1,0:T(8,128)(2,1)S(1)} %get-tuple-element.62), channel_id=1, source_target_pairs={{0,2},{1,3},{2,0},{3,1},{4,6},{5,7},{6,4},{7,5},{8,10},{9,11},{10,... | collective-permute-start | bytes 393224 | tf_op jit(solution)/shard_map/ppermute | solution.py:19
  75.4 20.2 %collective-permute-start.20 = (bf16[256,256]{1,0:T(8,128)(2,1)S(1)}, bf16[256,256]{1,0:T(8,128)(2,1)S(1)}, u32[]{:S(2)}, u32[]{:S(2)}) collective-permute-start(bf16[256,256]{1,0:T(8,128)(2,1)S(1)} %get-tuple-element.63), channel_id=1, source_target_pairs={{0,3},{1,2},{2,1},{3,0},{4,7},{5,6},{6,5},{7,4},{8,11},{9,10},{10,... | collective-permute-start | bytes 393224 | tf_op jit(solution)/shard_map/ppermute | solution.py:19
  78.6 19.1 %collective-permute-start.17 = (bf16[256,256]{1,0:T(8,128)(2,1)S(1)}, bf16[256,256]{1,0:T(8,128)(2,1)S(1)}, u32[]{:S(2)}, u32[]{:S(2)}) collective-permute-start(bf16[256,256]{1,0:T(8,128)(2,1)S(1)} %get-tuple-element.60), channel_id=1, source_target_pairs={{0,1},{1,0},{2,3},{3,2},{4,5},{5,4},{6,7},{7,6},{8,9},{9,8},{10,11... | collective-permute-start | bytes 393224 | tf_op jit(solution)/shard_map/ppermute | solution.py:19
  79.2 7.5 %collective-permute-start.25 = (bf16[64,256]{1,0:T(8,128)(2,1)S(1)}, bf16[64,256]{1,0:T(8,128)(2,1)S(1)}, u32[]{:S(2)}, u32[]{:S(2)}) collective-permute-start(bf16[64,256]{1,0:T(8,128)(2,1)S(1)} %get-tuple-element.71), channel_id=1, source_target_pairs={{0,1},{1,0},{2,3},{3,2},{4,5},{5,4},{6,7},{7,6},{8,9},{9,8},{10,11... | collective-permute-start | bytes 98312 | tf_op jit(solution)/shard_map/ppermute | solution.py:19
  80.9 7.6 %collective-permute-start.26 = (bf16[64,256]{1,0:T(8,128)(2,1)S(1)}, bf16[64,256]{1,0:T(8,128)(2,1)S(1)}, u32[]{:S(2)}, u32[]{:S(2)}) collective-permute-start(bf16[64,256]{1,0:T(8,128)(2,1)S(1)} %get-tuple-element.72), channel_id=1, source_target_pairs={{0,2},{1,3},{2,0},{3,1},{4,6},{5,7},{6,4},{7,5},{8,10},{9,11},{10,... | collective-permute-start | bytes 98312 | tf_op jit(solution)/shard_map/ppermute | solution.py:19
  86.8 15.5 %collective-permute-start.39 = (bf16[1,2,128,256]{3,2,1,0:T(8,128)(2,1)S(1)}, bf16[1,2,128,256]{3,2,1,0:T(8,128)(2,1)S(1)}, u32[]{:S(2)}, u32[]{:S(2)}) collective-permute-start(bf16[1,2,128,256]{3,2,1,0:T(8,128)(2,1)S(1)} %shard_map.149.refs_8_), channel_id=1, source_target_pairs={{0,4},{4,0},{8,12},{12,8},{16,20},{20,16},{24,28},{28,24},{1,5},{5... | collective-permute-start | bytes 393224 | tf_op jit(solution)/shard_map/ppermute | solution.py:19
  88.4 5.7 %collective-permute-start.27 = (bf16[64,256]{1,0:T(8,128)(2,1)S(1)}, bf16[64,256]{1,0:T(8,128)(2,1)S(1)}, u32[]{:S(2)}, u32[]{:S(2)}) collective-permute-start(bf16[64,256]{1,0:T(8,128)(2,1)S(1)} %get-tuple-element.73), channel_id=1, source_target_pairs={{0,3},{1,2},{2,1},{3,0},{4,7},{5,6},{6,5},{7,4},{8,11},{9,10},{10,... | collective-permute-start | bytes 98312 | tf_op jit(solution)/shard_map/ppermute | solution.py:19
  94.2 4.0 %collective-permute-start.28 = (bf16[64,256]{1,0:T(8,128)(2,1)S(1)}, bf16[64,256]{1,0:T(8,128)(2,1)S(1)}, u32[]{:S(2)}, u32[]{:S(2)}) collective-permute-start(bf16[64,256]{1,0:T(8,128)(2,1)S(1)} %shard_map.145.refs_0_), channel_id=1, source_target_pairs={{0,8},{4,12},{8,0},{12,4},{16,24},{20,28},{24,16},{28,20},{1,9},{5... | collective-permute-start | bytes 98312 | tf_op jit(solution)/shard_map/ppermute | solution.py:19
  95.0 3.9 %collective-permute-start.29 = (bf16[64,256]{1,0:T(8,128)(2,1)S(1)}, bf16[64,256]{1,0:T(8,128)(2,1)S(1)}, u32[]{:S(2)}, u32[]{:S(2)}) collective-permute-start(bf16[64,256]{1,0:T(8,128)(2,1)S(1)} %shard_map.145.refs_0_), channel_id=1, source_target_pairs={{0,16},{4,20},{8,24},{12,28},{16,0},{20,4},{24,8},{28,12},{1,17},{... | collective-permute-start | bytes 98312 | tf_op jit(solution)/shard_map/ppermute | solution.py:19
  95.6 4.8 %collective-permute-start.30 = (bf16[64,256]{1,0:T(8,128)(2,1)S(1)}, bf16[64,256]{1,0:T(8,128)(2,1)S(1)}, u32[]{:S(2)}, u32[]{:S(2)}) collective-permute-start(bf16[64,256]{1,0:T(8,128)(2,1)S(1)} %shard_map.145.refs_0_), channel_id=1, source_target_pairs={{0,24},{4,28},{8,16},{12,20},{16,8},{20,12},{24,0},{28,4},{1,25},{... | collective-permute-start | bytes 98312 | tf_op jit(solution)/shard_map/ppermute | solution.py:19
  97.7 4.5 %collective-permute-start.31 = (bf16[64,256]{1,0:T(8,128)(2,1)S(1)}, bf16[64,256]{1,0:T(8,128)(2,1)S(1)}, u32[]{:S(2)}, u32[]{:S(2)}) collective-permute-start(bf16[64,256]{1,0:T(8,128)(2,1)S(1)} %shard_map.145.refs_0_), channel_id=1, source_target_pairs={{0,4},{4,0},{8,12},{12,8},{16,20},{20,16},{24,28},{28,24},{1,5},{5... | collective-permute-start | bytes 98312 | tf_op jit(solution)/shard_map/ppermute | solution.py:19
  98.2 4.1 %collective-permute-start.32 = (bf16[64,256]{1,0:T(8,128)(2,1)S(1)}, bf16[64,256]{1,0:T(8,128)(2,1)S(1)}, u32[]{:S(2)}, u32[]{:S(2)}) collective-permute-start(bf16[64,256]{1,0:T(8,128)(2,1)S(1)} %collective-permute-done.28.refs_1_), channel_id=1, source_target_pairs={{0,4},{4,0},{8,12},{12,8},{16,20},{20,16},{24,28},{28,24},{1,5},{5... | collective-permute-start | bytes 98312 | tf_op jit(solution)/shard_map/ppermute | solution.py:19
  98.9 3.3 %collective-permute-start.33 = (bf16[64,256]{1,0:T(8,128)(2,1)S(1)}, bf16[64,256]{1,0:T(8,128)(2,1)S(1)}, u32[]{:S(2)}, u32[]{:S(2)}) collective-permute-start(bf16[64,256]{1,0:T(8,128)(2,1)S(1)} %collective-permute-done.29.refs_2_), channel_id=1, source_target_pairs={{0,4},{4,0},{8,12},{12,8},{16,20},{20,16},{24,28},{28,24},{1,5},{5... | collective-permute-start | bytes 98312 | tf_op jit(solution)/shard_map/ppermute | solution.py:19
  100.4 1.8 %collective-permute-start.34 = (bf16[64,256]{1,0:T(8,128)(2,1)S(1)}, bf16[64,256]{1,0:T(8,128)(2,1)S(1)}, u32[]{:S(2)}, u32[]{:S(2)}) collective-permute-start(bf16[64,256]{1,0:T(8,128)(2,1)S(1)} %collective-permute-done.30.refs_3_), channel_id=1, source_target_pairs={{0,4},{4,0},{8,12},{12,8},{16,20},{20,16},{24,28},{28,24},{1,5},{5... | collective-permute-start | bytes 98312 | tf_op jit(solution)/shard_map/ppermute | solution.py:19
  (1 other events, 0.9 us)
